TPU v7x, 32 devices: a whole 2x2x4 slice. The times are simulated.
32 devices in a mesh: dp: 8 (over z, y), group: 4 (over x, core).
Axes of the slice: x: 2, y: 2, z: 4, core: 2. Of those that a mesh axis runs over, the one named last changes fastest.
Arguments:
- query_feats: bfloat16 [4096, 4096], P(('dp', 'group')), may hold values from -45 to 45
- passage_feats: bfloat16 [4096, 4096], P(('dp', 'group')), may hold values from -45 to 45
- head: bfloat16 [4096, 1024], replicated, may hold values from -0.09375 to 0.09375
- neg_ids: int32 [4096, 7], P(('dp', 'group')), may hold values from 0 to 4095, as said below
Outputs:
- head_grad: float32 [4096, 1024], P(('dp', 'group'))
- query_loss: float32 [4096], P(('dp', 'group'))
Inputs may be any that keep to these rules, and one draw needn't show every extreme that they name: `neg_ids`: the 7 ids of a query name rows on 7 different devices, each with the query's group index and another dp index. Of the ids of one device's rows, at most 128 name rows of any one other device, and for every device some other device is named exactly 128 times.
All inputs are finite; a program needn't handle non-finite values.
Results may differ from a plain program's by a relative error of at most 0.0045.
The roundings to bfloat16 on the way count: a program that leaves them out, or rounds other values in their place, can miss the bound.
Values may be sent and summed in bfloat16 or wider, within the bound.
A program may use at most 128 MiB of HBM per device.

v0:
```python
import jax
import jax.numpy as jnp
from jax import lax
from jax.sharding import PartitionSpec as P

scaling_divisor = 0.05
levels = 15.0
epsilon = 1e-06


def quantize(projected, low_bound, high_bound):
    as_float = projected.astype(jnp.float32)
    step_size = (high_bound - low_bound) / levels
    level_pos = (as_float - low_bound) / step_size
    quantized = low_bound + step_size * (
        level_pos - jnp.sin(2.0 * jnp.pi * level_pos) / (2.0 * jnp.pi)
    )
    inverse = lax.rsqrt(jnp.sum(quantized * quantized, axis=-1, keepdims=True) + epsilon)
    return ((quantized * inverse).astype(jnp.bfloat16), quantized, inverse)


def norm_back(cotangent, quantized, inverse):
    inner_prod = jnp.sum(quantized * cotangent, axis=-1, keepdims=True)
    return (inverse * cotangent - quantized * inverse**3 * inner_prod).astype(jnp.bfloat16)


def block_loss(
    anchor_vector_entries, inbatch_vector_entries, difficult_distractor_vectors, pos_mask
):
    pairwise_cosine_scores = (
        lax.dot_general(
            anchor_vector_entries,
            inbatch_vector_entries,
            (((1,), (1,)), ((), ())),
            preferred_element_type=jnp.float32,
        )
        / scaling_divisor
    )
    difficult_distractor_scores = (
        jnp.einsum(
            "pgu,pu->pg",
            difficult_distractor_vectors,
            anchor_vector_entries,
            preferred_element_type=jnp.float32,
        )
        / scaling_divisor
    )
    positive = jnp.sum(pairwise_cosine_scores * pos_mask, axis=1)
    exp_batch = jnp.exp(pairwise_cosine_scores)
    batch_total = jnp.sum(exp_batch, axis=1)
    exp_pos = jnp.exp(positive)
    hard_exp = jnp.exp(difficult_distractor_scores)
    hard_total = exp_pos + jnp.sum(hard_exp, axis=1)
    query_loss = jnp.log(batch_total) - positive + jnp.log(hard_total) - positive
    inbatch_normalized_share = (
        exp_batch / batch_total[:, None] - pos_mask * (2.0 - exp_pos / hard_total)[:, None]
    ).astype(jnp.bfloat16)
    difficult_normalized_share = (hard_exp / hard_total[:, None]).astype(jnp.bfloat16)
    anchor_vector_derivative = (
        jnp.dot(
            inbatch_normalized_share, inbatch_vector_entries, preferred_element_type=jnp.float32
        )
        + jnp.einsum(
            "mz,mzh->mh",
            difficult_normalized_share,
            difficult_distractor_vectors,
            preferred_element_type=jnp.float32,
        )
    ) / scaling_divisor
    inbatch_vector_derivative = (
        lax.dot_general(
            inbatch_normalized_share,
            anchor_vector_entries,
            (((0,), (0,)), ((), ())),
            preferred_element_type=jnp.float32,
        )
        / scaling_divisor
    )
    difficult_distractor_derivative = (
        difficult_normalized_share.astype(jnp.float32)[:, :, None]
        * anchor_vector_entries.astype(jnp.float32)[:, None, :]
        / scaling_divisor
    ).astype(jnp.bfloat16)
    return (
        query_loss,
        anchor_vector_derivative,
        inbatch_vector_derivative,
        difficult_distractor_derivative,
    )


def body(query_feats, passage_feats, head, neg_ids):
    row_count = query_feats.shape[0]
    emb_width = head.shape[1]
    negatives = neg_ids.shape[1]
    dp_count = lax.axis_size("dp")
    group_count = lax.axis_size("group")
    other_count = dp_count - 1
    slot_total = negatives * row_count
    base_load = slot_total // other_count
    capacity = (
        base_load
        + min(1, slot_total % other_count)
        + max(0, min(base_load, row_count - base_load - 1))
    )
    proj_query = jnp.dot(query_feats, head, preferred_element_type=jnp.float32).astype(jnp.bfloat16)
    proj_pass = jnp.dot(passage_feats, head, preferred_element_type=jnp.float32).astype(
        jnp.bfloat16
    )
    col_high = jnp.maximum(jnp.max(proj_query, axis=0), jnp.max(proj_pass, axis=0)).astype(
        jnp.float32
    )
    col_low = jnp.minimum(jnp.min(proj_query, axis=0), jnp.min(proj_pass, axis=0)).astype(
        jnp.float32
    )
    owners = (neg_ids // (group_count * row_count)).reshape(-1)
    local_rows = (neg_ids % row_count).reshape(-1)
    onehot = (owners[:, None] == jnp.arange(dp_count, dtype=jnp.int32)[None, :]).astype(jnp.int32)
    before = jnp.cumsum(onehot, axis=0) - onehot
    slot_rank = jnp.sum(before * onehot, axis=1)
    slot_index = owners * capacity + slot_rank
    requests = (
        jnp.full((dp_count * capacity,), -1, jnp.int32)
        .at[slot_index]
        .set(local_rows)
        .reshape(dp_count, capacity)
    )
    incoming = lax.all_to_all(requests, "dp", split_axis=0, concat_axis=0, tiled=True)
    is_valid = incoming >= 0
    picked = jnp.maximum(incoming, 0)
    high_bound, neg_low = lax.pmax((col_high, -col_low), ("dp", "group"))
    low_bound, high_bound = (-neg_low, high_bound)
    own_pass = quantize(proj_pass, low_bound, high_bound)
    send_rows = own_pass[0]
    outgoing = jnp.where(is_valid[:, :, None], send_rows[picked], jnp.zeros((), jnp.bfloat16))
    fetched = lax.all_to_all(outgoing, "dp", split_axis=0, concat_axis=0, tiled=True)
    inbatch_vector_entries = lax.all_gather(send_rows, "group", axis=0, tiled=True)
    own_query = quantize(proj_query, low_bound, high_bound)
    difficult_distractor_vectors = fetched.reshape(dp_count * capacity, emb_width)[
        slot_index
    ].reshape(row_count, negatives, emb_width)
    group_pos = lax.axis_index("group")
    cand_count = group_count * row_count
    pos_mask = (
        jnp.arange(cand_count)[None, :] == (group_pos * row_count + jnp.arange(row_count))[:, None]
    ).astype(jnp.float32)
    (
        query_loss,
        anchor_vector_derivative,
        inbatch_vector_derivative,
        difficult_distractor_derivative,
    ) = block_loss(own_query[0], inbatch_vector_entries, difficult_distractor_vectors, pos_mask)
    batch_back = lax.psum_scatter(
        inbatch_vector_derivative, "group", scatter_dimension=0, tiled=True
    )
    returned = (
        jnp.zeros((dp_count * capacity, emb_width), jnp.bfloat16)
        .at[slot_index]
        .set(difficult_distractor_derivative.reshape(-1, emb_width))
    )
    arrived = lax.all_to_all(
        returned.reshape(dp_count, capacity, emb_width),
        "dp",
        split_axis=0,
        concat_axis=0,
        tiled=True,
    )
    gather_onehot = (jnp.arange(row_count)[:, None] == incoming.reshape(-1)[None, :]).astype(
        jnp.bfloat16
    )
    hard_back = jnp.dot(
        gather_onehot, arrived.reshape(-1, emb_width), preferred_element_type=jnp.float32
    )
    pass_grad = batch_back + hard_back
    dy_query = norm_back(anchor_vector_derivative, own_query[1], own_query[2])
    dy_pass = norm_back(pass_grad, own_pass[1], own_pass[2])
    contract = (((0,), (0,)), ((), ()))
    grad_shard = lax.psum_scatter(
        lax.dot_general(query_feats, dy_query, contract, preferred_element_type=jnp.float32)
        + lax.dot_general(passage_feats, dy_pass, contract, preferred_element_type=jnp.float32),
        ("dp", "group"),
        scatter_dimension=0,
        tiled=True,
    )
    return (grad_shard, query_loss)


def solution(mesh):
    return jax.shard_map(
        body,
        mesh=mesh,
        in_specs=(
            P(("dp", "group"), None),
            P(("dp", "group"), None),
            P(),
            P(("dp", "group"), None),
        ),
        out_specs=(P(("dp", "group"), None), P(("dp", "group"))),
        check_vma=False,
    )
```

profile of v0, /device:TPU:0, one launch (start us, length us, event | category | flops | bytes accessed | tf_op | source)
XLA Modules:
  0.0 432.3 jit_solution(13065944382984922990)
XLA Ops:
  11.7 5.8 %scatter_custom_fusion = s32[1024]{0:T(1024)} fusion(s32[896]{0:T(1024)S(1)} %fusion.22, s32[896]{0:T(1024)S(1)} %reshape.169, s32[]{:T(128)} %constant.73.clone.1), kind=kCustom, calls=%fused_computation.70 | custom fusion | bytes 4100 | tf_op jit(solution)/shard_map/scatter | solution.py:125
  17.6 7.3 %all-to-all-start = ((s32[8,1,128]{2,1,0:T(1,128)}), s32[8,1,128]{2,1,0:T(1,128)S(1)}, u32[]{:S(2)}, u32[]{:S(2)}) async-start(s32[8,1,128]{2,1,0:T(1,128)} %bitcast.3), calls=%async_computation | async-start | bytes 8192 | tf_op jit(solution)/shard_map/all_to_all | solution.py:128
  24.9 4.7 %fusion.26 = (bf16[1024]{0:T(1024)(128)(2,1)S(1)}, bf16[1024]{0:T(1024)(128)(2,1)S(1)}, bf16[128,1024]{1,0:T(8,128)(2,1)S(1)}) fusion(bf16[128,4096]{1,0:T(8,128)(2,1)S(1)} %copy-done, bf16[4096,1024]{1,0:T(8,128)(2,1)} %param.6), kind=kOutput, calls=%fused_computation.83 | convolution fusion | flops 1074132992 | bytes 9703424 | tf_op jit(solution)/shard_map/dot_general | solution.py:106
  29.6 4.8 %fusion.25 = (bf16[1024]{0:T(1024)(128)(2,1)S(1)}, bf16[1024]{0:T(1024)(128)(2,1)S(1)}, bf16[128,1024]{1,0:T(8,128)(2,1)S(1)}) fusion(bf16[128,4096]{1,0:T(8,128)(2,1)S(1)} %copy-done.3, bf16[4096,1024]{1,0:T(8,128)(2,1)} %param.6), kind=kOutput, calls=%fused_computation.82 | convolution fusion | flops 1074132992 | bytes 9703424 | tf_op jit(solution)/shard_map/dot_general | solution.py:107
  34.5 40.8 %all-reduce = (f32[1024]{0:T(1024)S(1)}, f32[1024]{0:T(1024)S(1)}) all-reduce(f32[1024]{0:T(1024)S(1)} %maximum_convert_fusion, f32[1024]{0:T(1024)S(1)} %convert_negate_fusion), channel_id=1, replica_groups=mesh['dp'=8,'group'=4] {'dp','group'}, use_global_device_ids=true, to_apply=%region_5.6 | all-reduce | flops 2048 | bytes 16384 | tf_op jit(solution)/shard_map/pmax | solution.py:131
  75.3 4.1 multiply_reduce_fusion.3
  79.4 4.5 %multiply_convert_fusion.3 = (bf16[128,1024]{1,0:T(8,128)(2,1)}, bf16[128,1024]{1,0:T(8,128)(2,1)S(1)}) fusion(f32[128]{0:T(128)S(1)} %get-tuple-element.41, bf16[128,1024]{1,0:T(8,128)(2,1)S(1)} %get-tuple-element.37, f32[1024]{0:T(1024)S(1)} %get-tuple-element.28, f32[1024]{0:T(1024)S(1)} %get-tuple-element.27, f32[128]{0:T(128)S(1)} %get-tuple-element.33, ...), kind=kLoop, calls=%fused_computation.27 | loop fusion | flops 2621440 | bytes 1057792 | tf_op jit(solution)/shard_map/convert_element_type | solution.py:19
  83.9 4.1 gather_fusion
  89.6 5.6 %all-to-all-start.1 = ((bf16[8,128,1024]{2,1,0:T(8,128)(2,1)}), bf16[8,128,1024]{2,1,0:T(8,128)(2,1)S(1)}, u32[]{:S(2)}, u32[]{:S(2)}) async-start(bf16[8,128,1024]{2,1,0:T(8,128)(2,1)} %broadcast_select_fusion), calls=%async_computation.1 | async-start | bytes 4194304 | tf_op jit(solution)/shard_map/all_to_all | solution.py:136
  96.1 18.6 %all-gather.2.cloned.1.call-done = bf16[512,1024]{1,0:T(8,128)(2,1)} async-done(((bf16[128,1024]{1,0:T(8,128)(2,1)}), bf16[512,1024]{1,0:T(8,128)(2,1)}) %all-gather.2.cloned.1.call-update) | async-done | bytes 1048592 | tf_op jit(solution)/shard_map/all_gather | solution.py:137
  114.7 2.4 exponential_reduce_fusion
  117.1 24.6 %all-to-all-done.1 = bf16[8,128,1024]{2,1,0:T(8,128)(2,1)S(1)} async-done(((bf16[8,128,1024]{2,1,0:T(8,128)(2,1)}), bf16[8,128,1024]{2,1,0:T(8,128)(2,1)S(1)}, u32[]{:S(2)}, u32[]{:S(2)}) %all-to-all-start.1) | async-done | bytes 2097184 | tf_op jit(solution)/shard_map/all_to_all | solution.py:136
  141.7 4.2 gather_fusion.1
  145.9 2.6 reshape.145
  152.4 2.5 mul.182
  154.8 5.0 %mul.183 = f32[896,1024]{1,0:T(8,128)} reshape(f32[128,7,1024]{2,1,0:T(8,128)} %mul.182) | data formatting | bytes 7340032 | tf_op jit(solution)/shard_map/mul | solution.py:80
  160.1 11.3 %scatter_custom_fusion.1 = bf16[1024,1024]{1,0:T(8,128)(2,1)} fusion(s32[896]{0:T(1024)S(1)} %fusion.22, f32[896,1024]{1,0:T(8,128)} %mul.183, f32[]{:T(128)} %constant.69.clone.1, f32[896]{0:T(1024)S(1)} %reshape.148, bf16[]{:T(256)} %constant.80.clone.1), kind=kCustom, calls=%fused_computation.7 | custom fusion | flops 2752512 | bytes 5771270 | tf_op jit(solution)/shard_map/scatter | solution.py:159
  171.4 4.3 %all-to-all-start.2 = ((bf16[8,128,1024]{2,1,0:T(8,128)(2,1)}), bf16[8,128,1024]{2,1,0:T(8,128)(2,1)}, u32[]{:S(2)}, u32[]{:S(2)}) async-start(bf16[8,128,1024]{2,1,0:T(8,128)(2,1)} %bitcast.48), calls=%async_computation.3 | async-start | bytes 4194304 | tf_op jit(solution)/shard_map/all_to_all | solution.py:161
  177.7 45.9 %all-to-all-done.2 = bf16[8,128,1024]{2,1,0:T(8,128)(2,1)} async-done(((bf16[8,128,1024]{2,1,0:T(8,128)(2,1)}), bf16[8,128,1024]{2,1,0:T(8,128)(2,1)}, u32[]{:S(2)}, u32[]{:S(2)}) %all-to-all-start.2) | async-done | bytes 2097184 | tf_op jit(solution)/shard_map/all_to_all | solution.py:161
  223.6 5.6 %multiply_reduce_fusion = (f32[128]{0:T(128)S(1)}, f32[128]{0:T(128)S(1)}, f32[128,1024]{1,0:T(8,128)S(1)}) fusion(bf16[128,1024]{1,0:T(8,128)(2,1)S(1)} %copy-done.6, f32[1024]{0:T(1024)S(1)} %get-tuple-element.28, f32[1024]{0:T(1024)S(1)} %get-tuple-element.27, f32[128,1024]{1,0:T(8,128)S(1)} %convolution_add_fusion, bf16[128,1024]{1,0:T(8,128)(2,1)S(1)} %copy-done.8, ...), kind=kOutput, calls=%fused_computation.20 | convolution fusion | flops 271449856 | bytes 4207616 | tf_op jit(solution)/shard_map/dot_general | solution.py:171
  229.3 4.2 fusion.6
  233.5 8.0 %add_bitcast_fusion = f32[4096,1024]{0,1:T(8,128)} fusion(f32[1024,4096]{1,0:T(8,128)S(1)} %fusion.6, bf16[128,4096]{1,0:T(8,128)(2,1)S(1)} %copy-done.4, f32[128,1024]{1,0:T(8,128)S(1)} %get-tuple-element.40, f32[128]{0:T(128)S(1)} %get-tuple-element.16, f32[128]{0:T(128)S(1)} %get-tuple-element.32, f32[128]{0:T(128)S(1)} %get-tuple-element.33, ...), kind=kOutput, calls=%fused_computation.4 | convolution fusion | flops 1079640064 | bytes 35399168 | tf_op jit(solution)/shard_map/dot_general | solution.py:180
  241.5 182.2 %reduce-scatter.5.cloned.1.call-done = f32[128,1024]{0,1:T(8,128)} async-done(((f32[4096,1024]{0,1:T(8,128)}), f32[128,1024]{0,1:T(8,128)}) %reduce-scatter.5.cloned.1.call-update) | async-done | bytes 524304 | tf_op jit(solution)/shard_map/reduce_scatter | solution.py:178
  423.7 2.0 copy.31
  (68 shorter events, 13.2 us)
Async XLA Ops:
  7.2 17.7 %copy-start = (bf16[128,4096]{1,0:T(8,128)(2,1)S(1)}, bf16[128,4096]{1,0:T(8,128)(2,1)}, u32[]{:S(2)}) copy-start(bf16[128,4096]{1,0:T(8,128)(2,1)} %param.4) | copy-start | bytes 3145732
  17.6 66.3 %all-to-all-start = ((s32[8,1,128]{2,1,0:T(1,128)}), s32[8,1,128]{2,1,0:T(1,128)S(1)}, u32[]{:S(2)}, u32[]{:S(2)}) async-start(s32[8,1,128]{2,1,0:T(1,128)} %bitcast.3), calls=%async_computation | async-start | bytes 8192 | tf_op jit(solution)/shard_map/all_to_all | solution.py:128
  24.9 4.8 %copy-start.3 = (bf16[128,4096]{1,0:T(8,128)(2,1)S(1)}, bf16[128,4096]{1,0:T(8,128)(2,1)}, u32[]{:S(2)}) copy-start(bf16[128,4096]{1,0:T(8,128)(2,1)} %param.5) | copy-start | bytes 3145732
  29.6 49.8 %copy-start.7 = (bf16[128,1024]{1,0:T(8,128)(2,1)}, bf16[128,1024]{1,0:T(8,128)(2,1)S(1)}, u32[]{:S(2)}) copy-start(bf16[128,1024]{1,0:T(8,128)(2,1)S(1)} %get-tuple-element.37) | copy-start | bytes 786436
  34.5 49.4 %copy-start.5 = (bf16[128,1024]{1,0:T(8,128)(2,1)}, bf16[128,1024]{1,0:T(8,128)(2,1)S(1)}, u32[]{:S(2)}) copy-start(bf16[128,1024]{1,0:T(8,128)(2,1)S(1)} %get-tuple-element.38) | copy-start | bytes 786436
  83.9 4.1 copy-start.2
  89.6 25.1 %copy-start.9 = (bf16[128,1024]{1,0:T(8,128)(2,1)S(1)}, bf16[128,1024]{1,0:T(8,128)(2,1)}, u32[]{:S(2)}) copy-start(bf16[128,1024]{1,0:T(8,128)(2,1)} %get-tuple-element.22) | copy-start | bytes 786436
  89.6 52.1 %all-to-all-start.1 = ((bf16[8,128,1024]{2,1,0:T(8,128)(2,1)}), bf16[8,128,1024]{2,1,0:T(8,128)(2,1)S(1)}, u32[]{:S(2)}, u32[]{:S(2)}) async-start(bf16[8,128,1024]{2,1,0:T(8,128)(2,1)} %broadcast_select_fusion), calls=%async_computation.1 | async-start | bytes 4194304 | tf_op jit(solution)/shard_map/all_to_all | solution.py:136
  95.1 19.6 %all-gather.2.cloned.1.call-start = ((), (), s32[]{:S(2)}) async-start(), calls=%async_computation.5 | async-start | bytes 1310720 | tf_op jit(solution)/shard_map/all_gather | solution.py:137
  95.9 127.8 %reduce-scatter.3.cloned.1.call-start = ((), (), s32[]{:S(2)}) async-start(), calls=%async_computation.6 | async-start | bytes 2621440 | tf_op jit(solution)/shard_map/reduce_scatter | solution.py:153
  148.5 1.9 copy-start.11
  171.4 52.2 %all-to-all-start.2 = ((bf16[8,128,1024]{2,1,0:T(8,128)(2,1)}), bf16[8,128,1024]{2,1,0:T(8,128)(2,1)}, u32[]{:S(2)}, u32[]{:S(2)}) async-start(bf16[8,128,1024]{2,1,0:T(8,128)(2,1)} %bitcast.48), calls=%async_computation.3 | async-start | bytes 4194304 | tf_op jit(solution)/shard_map/all_to_all | solution.py:161
  175.8 247.9 %reduce-scatter.5.cloned.1.call-start = ((), (), s32[]{:S(2)}) async-start(), calls=%async_computation.7 | async-start | bytes 17301504 | tf_op jit(solution)/shard_map/reduce_scatter | solution.py:178
  176.0 1.2 copy-start.10
  176.0 1.3 copy-start.12
  176.2 47.5 %copy-start.6 = (bf16[128,1024]{1,0:T(8,128)(2,1)S(1)}, bf16[128,1024]{1,0:T(8,128)(2,1)}, u32[]{:S(2)}) copy-start(bf16[128,1024]{1,0:T(8,128)(2,1)} %copy-done.5) | copy-start | bytes 786436
  177.3 46.3 %copy-start.8 = (bf16[128,1024]{1,0:T(8,128)(2,1)S(1)}, bf16[128,1024]{1,0:T(8,128)(2,1)}, u32[]{:S(2)}) copy-start(bf16[128,1024]{1,0:T(8,128)(2,1)} %copy-done.7) | copy-start | bytes 786436
  229.3 4.2 copy-start.4
  241.5 184.2 %copy-start.1 = (bf16[128,4096]{1,0:T(8,128)(2,1)S(1)}, bf16[128,4096]{1,0:T(8,128)(2,1)}, u32[]{:S(2)}) copy-start(bf16[128,4096]{1,0:T(8,128)(2,1)} %param.4) | copy-start | bytes 3145732
Sparse Core Ops, SparseCore 0:
  97.5 17.1 all-gather.1
  152.5 30.1 reduce-scatter.2
  241.6 182.0 reduce-scatter.4
where the time goes:
time: 433 us; the launch traced here: 432 us
  waiting for transfers between devices  272 us (63%)
  blocking collectives  40.8 us (9%)
  matrix products  34.1 us (8%)
  local copies, waits for them, and re-layouts  28.3 us (7%)
  other arithmetic  25.3 us (6%)
  starting transfers between devices  17.7 us (4%)
  between operations  14.1 us (3%)
    reduce_scatter x1, waiting for transfers between devices, body(): lax.psum_scatter(lax.dot_general(query_feats, dy_query, contract, preferr...  182 us
    all_to_all x1, waiting for transfers between devices, body(): lax.all_to_all(returned.reshape(dp_count, capacity, emb_width), 'dp', spl...  45.9 us
    pmax x1, blocking collectives, body(): high_bound, neg_low = lax.pmax((col_high, -col_low), ('dp', 'group'))  40.8 us
    all_to_all x1, waiting for transfers between devices, body(): lax.all_to_all(outgoing, 'dp', split_axis=0, concat_axis=0, tiled=True)  24.6 us
    all_gather x1, waiting for transfers between devices, body(): lax.all_gather(send_rows, 'group', axis=0, tiled=True)  18.6 us
    scatter x1, other arithmetic, body(): returned = jnp.zeros((dp_count * capacity, emb_width), jnp.bfloat16).at[s...  11.3 us
  transfers between devices with their start and end apart: 6, of which 4 were waited for; matrix products, arithmetic and copies ran while one was open for 9% of the time, Pallas kernels for 0%

commit v1 on v0

v1 whole, which is shorter than its diff:
```python
import functools

import jax
import jax.numpy as jnp
from jax import lax
from jax.experimental import pallas as pl
from jax.experimental.pallas import tpu as pltpu
from jax.sharding import PartitionSpec as P

scaling_divisor = 0.05
levels = 15.0
epsilon = 1e-06
MESH = pl.DeviceIdType.MESH
VMEM = pl.BlockSpec(memory_space=pltpu.VMEM)


def quantize(projected, low_bound, high_bound):
    as_float = projected.astype(jnp.float32)
    step_size = (high_bound - low_bound) / levels
    level_pos = (as_float - low_bound) / step_size
    quantized = low_bound + step_size * (
        level_pos - jnp.sin(2.0 * jnp.pi * level_pos) / (2.0 * jnp.pi)
    )
    inverse = lax.rsqrt(jnp.sum(quantized * quantized, axis=-1, keepdims=True) + epsilon)
    return ((quantized * inverse).astype(jnp.bfloat16), quantized, inverse)


def norm_back(cotangent, quantized, inverse):
    inner_prod = jnp.sum(quantized * cotangent, axis=-1, keepdims=True)
    return (inverse * cotangent - quantized * inverse**3 * inner_prod).astype(jnp.bfloat16)


def bounds_kernel(n_dp, n_group, own, out, from_group, from_dp, mid, send_g, recv_g, send_d, recv_d):
    me_d, me_g = lax.axis_index("dp"), lax.axis_index("group")

    def exchange(src, landing, send, recv, count, target):
        copies = []
        for k in range(1, count):
            copy = pltpu.make_async_remote_copy(
                src_ref=src,
                dst_ref=landing.at[k],
                send_sem=send.at[k],
                recv_sem=recv.at[k],
                device_id=target(k),
                device_id_type=MESH,
            )
            copy.start()
            copies.append(copy)
        for copy in copies:
            copy.wait()
        total = src[...]
        for k in range(1, count):
            total = jnp.maximum(total, landing[k])
        return total

    mid[...] = exchange(
        own, from_group, send_g, recv_g, n_group, lambda k: (me_d, lax.rem(me_g + k, n_group))
    )
    out[...] = exchange(
        mid, from_dp, send_d, recv_d, n_dp, lambda k: (lax.rem(me_d + k, n_dp), me_g)
    )


def all_bounds(own, n_dp, n_group):
    return pl.pallas_call(
        functools.partial(bounds_kernel, n_dp, n_group),
        out_shape=jax.ShapeDtypeStruct(own.shape, own.dtype),
        in_specs=[VMEM],
        out_specs=VMEM,
        scratch_shapes=[
            pltpu.VMEM((n_group,) + own.shape, own.dtype),
            pltpu.VMEM((n_dp,) + own.shape, own.dtype),
            pltpu.VMEM(own.shape, own.dtype),
            pltpu.SemaphoreType.DMA((n_group,)),
            pltpu.SemaphoreType.DMA((n_group,)),
            pltpu.SemaphoreType.DMA((n_dp,)),
            pltpu.SemaphoreType.DMA((n_dp,)),
        ],
        compiler_params=pltpu.CompilerParams(has_side_effects=True),
        name="bounds",
    )(own)


def dot_nt(a, b):
    return lax.dot_general(a, b, (((1,), (1,)), ((), ())), preferred_element_type=jnp.float32)


def dot_tn(a, b):
    return lax.dot_general(a, b, (((0,), (0,)), ((), ())), preferred_element_type=jnp.float32)


def body(query_feats, passage_feats, head, neg_ids):
    rows, width = query_feats.shape
    emb = head.shape[1]
    negatives = neg_ids.shape[1]
    n_dp = lax.axis_size("dp")
    n_group = lax.axis_size("group")
    block = width // (n_dp * n_group)
    me_g = lax.axis_index("group")

    feats = jnp.stack([query_feats, passage_feats]).reshape(2, rows, n_dp, n_group, block)
    feats = feats.transpose(3, 0, 1, 2, 4).reshape(n_group, 2 * rows, n_dp * block)
    feats = lax.all_to_all(feats, "group", split_axis=0, concat_axis=0, tiled=True)
    feats = feats.reshape(n_group * 2 * rows, n_dp * block)

    proj_query = jnp.dot(query_feats, head, preferred_element_type=jnp.float32).astype(jnp.bfloat16)
    proj_pass = jnp.dot(passage_feats, head, preferred_element_type=jnp.float32).astype(
        jnp.bfloat16
    )
    col_high = jnp.maximum(jnp.max(proj_query, axis=0), jnp.max(proj_pass, axis=0)).astype(
        jnp.float32
    )
    col_low = jnp.minimum(jnp.min(proj_query, axis=0), jnp.min(proj_pass, axis=0)).astype(
        jnp.float32
    )
    bounds = all_bounds(jnp.stack([col_high, -col_low]), n_dp, n_group)
    high_bound, low_bound = bounds[0], -bounds[1]

    query, quant_query, inv_query = quantize(proj_query, low_bound, high_bound)
    passage, quant_pass, inv_pass = quantize(proj_pass, low_bound, high_bound)
    batch_pass = lax.all_gather(passage, "group", axis=0, tiled=True)
    dp_pass = lax.all_gather(passage, "dp", axis=0, tiled=True)
    batch_query = lax.all_gather(query, "group", axis=0, tiled=True)
    dp_query = lax.all_gather(query, "dp", axis=0, tiled=True)

    named = (neg_ids // (n_group * rows)) * rows + neg_ids % rows
    places = jnp.arange(n_dp * rows, dtype=jnp.int32)[None, :]
    is_hard = named[:, 0:1] == places
    for k in range(1, negatives):
        is_hard = is_hard | (named[:, k : k + 1] == places)

    pos_mask = (
        jnp.arange(n_group * rows)[None, :] == (me_g * rows + jnp.arange(rows))[:, None]
    ).astype(jnp.float32)
    scores = dot_nt(query, batch_pass) / scaling_divisor
    hard_scores = dot_nt(query, dp_pass) / scaling_divisor
    positive = jnp.sum(scores * pos_mask, axis=1)
    exp_batch = jnp.exp(scores)
    batch_total = jnp.sum(exp_batch, axis=1)
    exp_pos = jnp.exp(positive)
    hard_exp = jnp.where(is_hard, jnp.exp(hard_scores), 0.0)
    hard_total = exp_pos + jnp.sum(hard_exp, axis=1)
    query_loss = jnp.log(batch_total) - positive + jnp.log(hard_total) - positive
    batch_weight = (
        exp_batch / batch_total[:, None] - pos_mask * (2.0 - exp_pos / hard_total)[:, None]
    ).astype(jnp.bfloat16)
    hard_weight = (hard_exp / hard_total[:, None]).astype(jnp.bfloat16)

    batch_arrived = lax.all_to_all(batch_weight, "group", split_axis=1, concat_axis=0, tiled=True)
    hard_arrived = lax.all_to_all(hard_weight, "dp", split_axis=1, concat_axis=0, tiled=True)

    query_grad = (
        jnp.dot(batch_weight, batch_pass, preferred_element_type=jnp.float32)
        + jnp.dot(hard_weight, dp_pass, preferred_element_type=jnp.float32)
    ) / scaling_divisor
    dy_query = norm_back(query_grad, quant_query, inv_query)

    one_weight = jnp.sum(hard_arrived.astype(jnp.float32), axis=1, keepdims=True)
    hard_grad = (one_weight * dp_query.astype(jnp.float32) / scaling_divisor).astype(jnp.bfloat16)
    chosen = (hard_arrived != 0).astype(jnp.bfloat16)
    pass_grad = dot_tn(batch_arrived, batch_query) / scaling_divisor + dot_tn(chosen, hard_grad)
    dy_pass = norm_back(pass_grad, quant_pass, inv_pass)

    dy = lax.all_gather(jnp.concatenate([dy_query, dy_pass]), "group", axis=0, tiled=True)
    partial = dot_tn(feats, dy).astype(jnp.bfloat16).reshape(n_dp, block, emb)
    shares = lax.all_to_all(partial, "dp", split_axis=0, concat_axis=0, tiled=True)
    head_grad = jnp.sum(shares.astype(jnp.float32), axis=0)
    return (head_grad, query_loss)


def solution(mesh):
    return jax.shard_map(
        body,
        mesh=mesh,
        in_specs=(
            P(("dp", "group"), None),
            P(("dp", "group"), None),
            P(),
            P(("dp", "group"), None),
        ),
        out_specs=(P(("dp", "group"), None), P(("dp", "group"))),
        check_vma=False,
    )
```

time: 433 us -> 299 us (0.69)
  waiting for transfers between devices: 272 us -> 114 us
  blocking collectives: 40.8 us -> 92.9 us
  local copies, waits for them, and re-layouts: 28.3 us -> 5.4 us
  Pallas kernels: 0 us -> 18 us
  starting transfers between devices: 17.7 us -> 7.11 us
  other arithmetic: 25.3 us -> 18.6 us
  matrix products: 34.1 us -> 28.1 us
    reduce_scatter x2 -> x0, waiting for transfers between devices: 182 us -> none  [the longest x1 182 us: body(): lax.psum_scatter(lax.dot_general(query_feats, dy_query, contract, preferr...]
    all_to_all x0 -> x2, blocking collectives: none -> 92.9 us  [the longest x1 53.6 us: body(): lax.all_to_all(partial, 'dp', split_axis=0, concat_axis=0, tiled=True)]
    all_gather x1 -> x5, waiting for transfers between devices: 18.6 us -> 101 us  [the longest x1 49.9 us: body(): dp_pass = lax.all_gather(passage, 'dp', axis=0, tiled=True)]
    all_to_all x3 -> x2, waiting for transfers between devices: 70.5 us -> 10.2 us  [the longest x1 10.2 us: body(): lax.all_to_all(hard_weight, 'dp', split_axis=1, concat_axis=0, tiled=True)]
    pmax x1 -> x0, blocking collectives: 40.8 us -> none  [body(): high_bound, neg_low = lax.pmax((col_high, -col_low), ('dp', 'group'))]
    pallas_call x0 -> x1, Pallas kernels: none -> 18 us  [all_bounds(): pl.pallas_call(functools.partial(bounds_kernel, n_dp, n_group), out_shape...]
    scatter x1 -> x0, other arithmetic: 11.3 us -> none  [body(): returned = jnp.zeros((dp_count * capacity, emb_width), jnp.bfloat16).at[s...]
    all_to_all x3 -> x2, starting transfers between devices: 17.2 us -> 6.74 us  [the longest x1 3.41 us: body(): lax.all_to_all(hard_weight, 'dp', split_axis=1, concat_axis=0, tiled=True)]
  transfers between devices with their start and end apart: 6 -> 7, of which waited for: 4 -> 5; matrix products, arithmetic and copies ran while one was open for 9% -> 6% of each run, Pallas kernels for 0% -> 0%
where the time goes in v1:
time: 299 us; the launch traced here: 298 us
  waiting for transfers between devices  114 us (38%)
  blocking collectives  92.9 us (31%)
  matrix products  28.1 us (9%)
  other arithmetic  18.6 us (6%)
  Pallas kernels  18 us (6%)
  between operations  14 us (5%)
  starting transfers between devices  7.11 us (2%)
  local copies, waits for them, and re-layouts  5.4 us (2%)
    all_to_all x1, blocking collectives, body(): lax.all_to_all(partial, 'dp', split_axis=0, concat_axis=0, tiled=True)  53.6 us
    all_gather x1, waiting for transfers between devices, body(): dp_pass = lax.all_gather(passage, 'dp', axis=0, tiled=True)  49.9 us
    all_to_all x1, blocking collectives, body(): lax.all_to_all(feats, 'group', split_axis=0, concat_axis=0, tiled=True)  39.3 us
    all_gather x1, waiting for transfers between devices, body(): dp_query = lax.all_gather(query, 'dp', axis=0, tiled=True)  26.4 us
    pallas_call x1, Pallas kernels, all_bounds(): pl.pallas_call(functools.partial(bounds_kernel, n_dp, n_group), out_shape...  18 us
    all_gather x1, waiting for transfers between devices, body(): batch_query = lax.all_gather(query, 'group', axis=0, tiled=True)  13.4 us
    all_gather x1, waiting for transfers between devices, body(): batch_pass = lax.all_gather(passage, 'group', axis=0, tiled=True)  11.7 us
    all_to_all x1, waiting for transfers between devices, body(): lax.all_to_all(hard_weight, 'dp', split_axis=1, concat_axis=0, tiled=True)  10.2 us
  transfers between devices with their start and end apart: 7, of which 5 were waited for; matrix products, arithmetic and copies ran while one was open for 6% of the time, Pallas kernels for 0%

profile of v1, /device:TPU:0, one launch (start us, length us, event | category | flops | bytes accessed | tf_op | source)
XLA Modules:
  0.0 297.8 jit_solution(13261512712843139570)
XLA Ops:
  7.2 5.1 %fusion.18 = (bf16[1024]{0:T(1024)(128)(2,1)S(1)}, bf16[1024]{0:T(1024)(128)(2,1)S(1)}, bf16[128,1024]{1,0:T(8,128)(2,1)S(1)}) fusion(bf16[128,4096]{1,0:T(8,128)(2,1)} %param.5, bf16[4096,1024]{1,0:T(8,128)(2,1)} %param.6), kind=kOutput, calls=%fused_computation.83 | convolution fusion | flops 1074132992 | bytes 9703424 | tf_op jit(solution)/shard_map/dot_general | solution.py:107
  12.4 1.2 copy-done
  13.6 1.4 fusion.19
  15.6 18.0 %bounds.1 = f32[2,1024]{1,0:T(2,128)} custom-call(f32[2,1024]{1,0:T(2,128)} %pad_maximum_fusion.1.own), custom_call_target="tpu_custom_call" | custom-call | tf_op jit(solution)/shard_map/bounds/pallas_call | solution.py:65
  34.4 4.1 %multiply_reduce_fusion.2 = (f32[128]{0:T(128)S(1)}, f32[128]{0:T(128)S(1)}) fusion(bf16[128,1024]{1,0:T(8,128)(2,1)S(1)} %get-tuple-element.34, f32[1024]{0:T(1024)S(1)} %bitcast.68, f32[1024]{0:T(1024)S(1)} %bitcast.64, bf16[128,1024]{1,0:T(8,128)(2,1)S(1)} %get-tuple-element.33), kind=kLoop, calls=%fused_computation.31 | loop fusion | flops 2621184 | bytes 533504 | tf_op jit(solution)/shard_map/reduce_sum | solution.py:24
  38.5 4.5 %multiply_convert_fusion.2 = (bf16[128,1024]{1,0:T(8,128)(2,1)}, bf16[128,1024]{1,0:T(8,128)(2,1)}) fusion(f32[128]{0:T(128)S(1)} %get-tuple-element.32, bf16[128,1024]{1,0:T(8,128)(2,1)S(1)} %get-tuple-element.34, f32[1024]{0:T(1024)S(1)} %bitcast.69, f32[1024]{0:T(1024)S(1)} %bitcast.65, f32[128]{0:T(128)S(1)} %get-tuple-element.39, ...), kind=kLoop, calls=%fused_computation.30 | loop fusion | flops 2621440 | bytes 1057792 | tf_op jit(solution)/shard_map/convert_element_type | solution.py:25
  45.2 11.7 %all-gather.6.cloned.1.call-done = bf16[512,1024]{1,0:T(8,128)(2,1)} async-done(((bf16[128,1024]{1,0:T(8,128)(2,1)}), bf16[512,1024]{1,0:T(8,128)(2,1)}) %all-gather.6.cloned.1.call-update) | async-done | bytes 1048592 | tf_op jit(solution)/shard_map/all_gather | solution.py:121
  56.9 1.9 exponential_reduce_fusion
  58.8 49.9 %all-gather.8.cloned.1.call-done = bf16[1024,1024]{1,0:T(8,128)(2,1)} async-done(((bf16[128,1024]{1,0:T(8,128)(2,1)}), bf16[1024,1024]{1,0:T(8,128)(2,1)}) %all-gather.8.cloned.1.call-update) | async-done | bytes 2097168 | tf_op jit(solution)/shard_map/all_gather | solution.py:122
  108.7 2.7 fusion.20
  112.8 3.4 %all-to-all-start.2 = ((bf16[128,8,128]{2,0,1:T(8,128)(2,1)}), bf16[128,8,128]{2,0,1:T(8,128)(2,1)S(1)}, u32[]{:S(2)}, u32[]{:S(2)}) async-start(bf16[128,8,128]{2,0,1:T(8,128)(2,1)} %copy_bitcast_fusion), calls=%async_computation.2 | async-start | bytes 524288 | tf_op jit(solution)/shard_map/all_to_all | solution.py:150
  117.0 3.0 fusion.21
  120.0 10.2 %all-to-all-done.2 = bf16[128,8,128]{2,0,1:T(8,128)(2,1)S(1)} async-done(((bf16[128,8,128]{2,0,1:T(8,128)(2,1)}), bf16[128,8,128]{2,0,1:T(8,128)(2,1)S(1)}, u32[]{:S(2)}, u32[]{:S(2)}) %all-to-all-start.2) | async-done | bytes 262176 | tf_op jit(solution)/shard_map/all_to_all | solution.py:150
  130.2 3.3 %all-to-all-start.1 = ((bf16[128,4,128]{2,0,1:T(8,128)(2,1)}), bf16[128,4,128]{2,0,1:T(8,128)(2,1)S(1)}, u32[]{:S(2)}, u32[]{:S(2)}) async-start(bf16[128,4,128]{2,0,1:T(8,128)(2,1)} %copy_bitcast_fusion.1), calls=%async_computation.1 | async-start | bytes 262144 | tf_op jit(solution)/shard_map/all_to_all | solution.py:149
  134.0 26.4 %all-gather.12.cloned.1.call-done = bf16[1024,1024]{1,0:T(8,128)(2,1)} async-done(((bf16[128,1024]{1,0:T(8,128)(2,1)}), bf16[1024,1024]{1,0:T(8,128)(2,1)}) %all-gather.12.cloned.1.call-update) | async-done | bytes 2097168 | tf_op jit(solution)/shard_map/all_gather | solution.py:124
  160.4 3.2 %fusion = f32[128,1024]{1,0:T(8,128)} fusion(pred[1024,128]{1,0:T(32,128)(4,1)S(1)} %bitcast.63, bf16[1024,1024]{1,0:T(8,128)(2,1)} %all-gather.12.cloned.1.call-done, f32[1024]{0:T(1024)S(1)} %bitcast.74), kind=kOutput, calls=%fused_computation.2 | convolution fusion | flops 272629760 | bytes 2756608 | tf_op jit(solution)/shard_map/dot_general | solution.py:89
  163.7 13.4 %all-gather.10.cloned.1.call-done = bf16[512,1024]{1,0:T(8,128)(2,1)} async-done(((bf16[128,1024]{1,0:T(8,128)(2,1)}), bf16[512,1024]{1,0:T(8,128)(2,1)}) %all-gather.10.cloned.1.call-update) | async-done | bytes 1048592 | tf_op jit(solution)/shard_map/all_gather | solution.py:123
  177.1 1.7 fusion.3
  178.8 5.1 %multiply_reduce_fusion.1 = (f32[128]{0:T(128)S(1)}, f32[128]{0:T(128)S(1)}, f32[128,1024]{1,0:T(8,128)S(1)}) fusion(bf16[128,1024]{1,0:T(8,128)(2,1)S(1)} %get-tuple-element.33, f32[1024]{0:T(1024)S(1)} %bitcast.70, f32[1024]{0:T(1024)S(1)} %bitcast.66, f32[128,1024]{1,0:T(8,128)S(1)} %fusion.3, bf16[128,1024]{1,0:T(8,128)(2,1)S(1)} %get-tuple-element.34, ...), kind=kOutput, calls=%fused_computation.21 | convolution fusion | flops 137428736 | bytes 3418624 | tf_op jit(solution)/shard_map/dot_general | solution.py:153
  183.9 4.0 %subtract_convert_fusion.1 = (bf16[128,1024]{1,0:T(8,128)(2,1)S(1)}, bf16[128,1024]{1,0:T(8,128)(2,1)S(1)}) fusion(f32[128,1024]{1,0:T(8,128)S(1)} %get-tuple-element.38, f32[128]{0:T(128)S(1)} %get-tuple-element.8, f32[128]{0:T(128)S(1)} %get-tuple-element.40, f32[128]{0:T(128)S(1)} %get-tuple-element.41, bf16[128,1024]{1,0:T(8,128)(2,1)S(1)} %get-tuple-element.33, ...), kind=kLoop, calls=%fused_computation.20 | loop fusion | flops 3407872 | bytes 2108416 | tf_op jit(solution)/shard_map/convert_element_type | solution.py:30
  190.9 2.3 reshape.109
  193.3 39.3 %all_to_all.42 = bf16[4,256,1024]{2,1,0:T(8,128)(2,1)S(1)} all-to-all(bf16[4,256,1024]{2,1,0:T(8,128)(2,1)} %reshape.109), channel_id=1, replica_groups=mesh['dp'=8,'group'=4] {'group'}, dimensions={0} | all-to-all | bytes 4194304 | tf_op jit(solution)/shard_map/all_to_all | solution.py:103
  232.5 4.0 %convolution_convert_fusion = bf16[1024,1024]{1,0:T(8,128)(2,1)S(1)} fusion(bf16[1024,1024]{1,0:T(8,128)(2,1)S(1)} %bitcast.60, bf16[1024,1024]{1,0:T(8,128)(2,1)} %all-gather.14.cloned.1.call-done), kind=kOutput, calls=%fused_computation.6 | convolution fusion | flops 2148532224 | bytes 6291456 | tf_op jit(solution)/shard_map/dot_general | solution.py:89
  236.5 53.6 %all_to_all.43 = bf16[8,128,1024]{2,1,0:T(8,128)(2,1)S(1)} all-to-all(bf16[8,128,1024]{2,1,0:T(8,128)(2,1)S(1)} %bitcast.61), channel_id=1, replica_groups=mesh['dp'=8,'group'=4] {'dp'}, dimensions={0} | all-to-all | bytes 4194304 | tf_op jit(solution)/shard_map/all_to_all | solution.py:166
  (43 shorter events, 10.1 us)
Async XLA Ops:
  7.2 5.2 %copy-start.1 = (bf16[128,4096]{1,0:T(8,128)(2,1)S(1)}, bf16[128,4096]{1,0:T(8,128)(2,1)}, u32[]{:S(2)}) copy-start(bf16[128,4096]{1,0:T(8,128)(2,1)} %param.4) | copy-start | bytes 3145732
  7.2 49.7 %all-gather.6.cloned.1.call-start = ((), (), s32[]{:S(2)}) async-start(), calls=%async_computation.4 | async-start | bytes 1310720 | tf_op jit(solution)/shard_map/all_gather | solution.py:121
  7.2 6.4 %copy-start = (bf16[4096,1024]{1,0:T(8,128)(2,1)S(1)}, bf16[4096,1024]{1,0:T(8,128)(2,1)}, u32[]{:S(2)}) copy-start(bf16[4096,1024]{1,0:T(8,128)(2,1)} %param.6) | copy-start | bytes 25165828
  15.0 30.2 %copy-start.5 = (s32[128,7]{0,1:T(8,128)S(1)}, s32[128,7]{0,1:T(8,128)}, u32[]{:S(2)}) copy-start(s32[128,7]{0,1:T(8,128)} %param.7) | copy-start | bytes 10756
  43.0 65.7 %copy-start.3 = (bf16[128,1024]{1,0:T(8,128)(2,1)S(1)}, bf16[128,1024]{1,0:T(8,128)(2,1)}, u32[]{:S(2)}) copy-start(bf16[128,1024]{1,0:T(8,128)(2,1)} %get-tuple-element.15) | copy-start | bytes 786436
  43.0 65.6 %all-gather.8.cloned.1.call-start = ((), (), s32[]{:S(2)}) async-start(), calls=%async_computation.5 | async-start | bytes 2359296 | tf_op jit(solution)/shard_map/all_gather | solution.py:122
  43.8 116.6 %all-gather.12.cloned.1.call-start = ((), (), s32[]{:S(2)}) async-start(), calls=%async_computation.7 | async-start | bytes 2359296 | tf_op jit(solution)/shard_map/all_gather | solution.py:124
  44.5 132.6 %all-gather.10.cloned.1.call-start = ((), (), s32[]{:S(2)}) async-start(), calls=%async_computation.6 | async-start | bytes 1310720 | tf_op jit(solution)/shard_map/all_gather | solution.py:123
  112.8 17.4 %all-to-all-start.2 = ((bf16[128,8,128]{2,0,1:T(8,128)(2,1)}), bf16[128,8,128]{2,0,1:T(8,128)(2,1)S(1)}, u32[]{:S(2)}, u32[]{:S(2)}) async-start(bf16[128,8,128]{2,0,1:T(8,128)(2,1)} %copy_bitcast_fusion), calls=%async_computation.2 | async-start | bytes 524288 | tf_op jit(solution)/shard_map/all_to_all | solution.py:150
  130.2 46.9 %all-to-all-start.1 = ((bf16[128,4,128]{2,0,1:T(8,128)(2,1)}), bf16[128,4,128]{2,0,1:T(8,128)(2,1)S(1)}, u32[]{:S(2)}, u32[]{:S(2)}) async-start(bf16[128,4,128]{2,0,1:T(8,128)(2,1)} %copy_bitcast_fusion.1), calls=%async_computation.1 | async-start | bytes 262144 | tf_op jit(solution)/shard_map/all_to_all | solution.py:149
  133.5 99.0 %all-gather.14.cloned.1.call-start = ((), (), s32[]{:S(2)}) async-start(), calls=%async_computation.8 | async-start | bytes 2621440 | tf_op jit(solution)/shard_map/all_gather | solution.py:164
  163.7 15.1 %copy-start.4 = (bf16[512,1024]{1,0:T(8,128)(2,1)S(1)}, bf16[512,1024]{1,0:T(8,128)(2,1)}, u32[]{:S(2)}) copy-start(bf16[512,1024]{1,0:T(8,128)(2,1)} %all-gather.6.cloned.1.call-done) | copy-start | bytes 3145732
  188.0 1.6 copy-start.2
Sparse Core Ops, SparseCore 0:
  43.2 13.6 all-gather.5
  59.6 49.0 all-gather.7
  110.8 49.5 all-gather.11
  161.8 15.2 all-gather.9
  189.0 32.7 all-gather.13

commit v2 on v1

--- a/solution.py
+++ b/solution.py
@@ -81,6 +81,267 @@
     )(own)
 
 
+def remote(src, dst, send, recv, device):
+    return pltpu.make_async_remote_copy(
+        src_ref=src,
+        dst_ref=dst,
+        send_sem=send,
+        recv_sem=recv,
+        device_id=device,
+        device_id_type=MESH,
+    )
+
+
+def gather_kernel(
+    n_dp, n_group, inner, passage, query, feats,
+    batch_pass, dp_pass, batch_query, dp_query, feats_out,
+    send_line, send_pair, recv_dp, send_group, recv_group, local_sem,
+):
+    me_d, me_g = lax.axis_index("dp"), lax.axis_index("group")
+    line = n_dp // inner
+    z, y = me_d // inner, lax.rem(me_d, inner)
+    items = ((passage, batch_pass, dp_pass), (query, batch_query, dp_query))
+
+    def slot_copy(i, source, src, send, target):
+        return remote(src, items[i][2].at[source], send, recv_dp.at[i, source], (target, me_g))
+
+    def forwards(i, at, src, rightward, leftward):
+        source = at * inner + y
+        copies = []
+        if rightward:
+            copies.append(
+                (z < line - 1, slot_copy(i, source, src, send_line.at[i, 0, at], lax.rem(me_d + inner, n_dp)))
+            )
+        if leftward:
+            copies.append(
+                (z > 0, slot_copy(i, source, src, send_line.at[i, 1, at], lax.rem(me_d + n_dp - inner, n_dp)))
+            )
+        for k in range(1, inner):
+            target = z * inner + lax.rem(y + k, inner)
+            copies.append((None, slot_copy(i, source, src, send_pair.at[i, k, at], target)))
+        return copies
+
+    def each(copies, act):
+        for condition, copy in copies:
+            if condition is None:
+                act(copy)
+            else:
+                pl.when(condition)(functools.partial(act, copy))
+
+    def start(copy):
+        copy.start()
+
+    def wait_send(copy):
+        copy.wait_send()
+
+    def group_copy(j, src, dst, k):
+        target = lax.rem(me_g + k, n_group)
+        return remote(
+            src(target), dst.at[me_g], send_group.at[j, k], recv_group.at[j, k], (me_d, target)
+        )
+
+    def group_copies(j, k):
+        if j < 2:
+            return group_copy(j, lambda target: items[j][0], items[j][1], k)
+        return group_copy(j, lambda target: feats.at[target], feats_out, k)
+
+    for i in range(2):
+        each(forwards(i, z, items[i][0], True, True), start)
+        for k in range(1, n_group):
+            group_copies(i, k).start()
+    for k in range(1, n_group):
+        group_copies(2, k).start()
+    local = []
+    for i, (own, batch, over_dp) in enumerate(items):
+        local.append(pltpu.make_async_copy(own, batch.at[me_g], local_sem.at[2 * i]))
+        local.append(pltpu.make_async_copy(own, over_dp.at[me_d], local_sem.at[2 * i + 1]))
+    local.append(pltpu.make_async_copy(feats.at[me_g], feats_out.at[me_g], local_sem.at[4]))
+    for copy in local:
+        copy.start()
+
+    for s in range(1, line):
+        for i in range(2):
+            for at, inside, onward in ((z - s, z >= s, True), (z + s, z + s < line, False)):
+
+                @pl.when(inside)
+                def _(i=i, at=at, onward=onward):
+                    source = at * inner + y
+                    block = items[i][2].at[source]
+                    slot_copy(i, source, block, send_line.at[i, 0, at], me_d).wait_recv()
+                    each(forwards(i, at, block, onward, not onward), start)
+
+    for i in range(2):
+        for k in range(1, inner):
+            for at in range(line):
+                source = at * inner + lax.rem(y + k, inner)
+                block = items[i][2].at[source]
+                slot_copy(i, source, block, send_pair.at[i, k, at], me_d).wait_recv()
+        each(forwards(i, z, items[i][0], True, True), wait_send)
+    for s in range(1, line):
+        for i in range(2):
+            for at, inside, onward in ((z - s, z >= s, True), (z + s, z + s < line, False)):
+
+                @pl.when(inside)
+                def _(i=i, at=at, onward=onward):
+                    block = items[i][2].at[at * inner + y]
+                    each(forwards(i, at, block, onward, not onward), wait_send)
+
+    for j in range(3):
+        for k in range(1, n_group):
+            group_copies(j, k).wait_send()
+            dst = (batch_pass, batch_query, feats_out)[j]
+            landed = dst.at[lax.rem(me_g + n_group - k, n_group)]
+            remote(
+                landed, landed, send_group.at[j, k], recv_group.at[j, k], (me_d, me_g)
+            ).wait_recv()
+    for copy in local:
+        copy.wait()
+
+
+def gather_all(passage, query, feats, n_dp, n_group):
+    inner = 2 if n_dp % 2 == 0 else 1
+    line = n_dp // inner
+    dtype = passage.dtype
+    over = lambda n: jax.ShapeDtypeStruct((n,) + passage.shape, dtype)
+    anywhere = pl.BlockSpec(memory_space=pl.ANY)
+    return pl.pallas_call(
+        functools.partial(gather_kernel, n_dp, n_group, inner),
+        out_shape=(
+            over(n_group), over(n_dp), over(n_group), over(n_dp),
+            jax.ShapeDtypeStruct(feats.shape, dtype),
+        ),
+        in_specs=[VMEM] * 3,
+        out_specs=(anywhere,) * 5,
+        scratch_shapes=[
+            pltpu.SemaphoreType.DMA((2, 2, line)),
+            pltpu.SemaphoreType.DMA((2, inner, line)),
+            pltpu.SemaphoreType.DMA((2, n_dp)),
+            pltpu.SemaphoreType.DMA((3, n_group)),
+            pltpu.SemaphoreType.DMA((3, n_group)),
+            pltpu.SemaphoreType.DMA((5,)),
+        ],
+        compiler_params=pltpu.CompilerParams(has_side_effects=True),
+        name="gather",
+    )(passage, query, feats)
+
+
+def reduce_kernel(
+    n_dp, n_group, inner, chunks, dy, feats, out,
+    turned, gathered, total, pair_out, pair_in, line_out, line_in, kept,
+    send_g, recv_g, send_p, recv_p, send_l, recv_l,
+):
+    me_d, me_g = lax.axis_index("dp"), lax.axis_index("group")
+    line = n_dp // inner
+    z, y = me_d // inner, lax.rem(me_d, inner)
+    tokens, emb = dy.shape
+    wide = emb // chunks
+    block = out.shape[0]
+    columns = lambda c: pl.ds(c * wide, wide)
+
+    def dy_copy(c, k):
+        target = lax.rem(me_g + k, n_group)
+        return remote(
+            dy.at[:, columns(c)], gathered.at[k, :, columns(c)],
+            send_g.at[c, k], recv_g.at[c, k], (me_d, target),
+        )
+
+    def pair_copy(c, k):
+        target = z * inner + lax.rem(y + k, inner)
+        return remote(
+            pair_out.at[c, k], pair_in.at[c, k], send_p.at[c, k], recv_p.at[c, k], (target, me_g)
+        )
+
+    def line_copy(c, j):
+        target = lax.rem(z + j, line) * inner + y
+        return remote(
+            line_out.at[c, j], line_in.at[c, j], send_l.at[c, j], recv_l.at[c, j], (target, me_g)
+        )
+
+    for c in range(chunks):
+        for k in range(1, n_group):
+            dy_copy(c, k).start()
+    for k in range(n_group):
+        turned[k] = feats[lax.rem(me_g + n_group - k, n_group)].T
+
+    def first(c):
+        part = jnp.dot(turned[0], dy[:, columns(c)], preferred_element_type=jnp.float32)
+        for k in range(1, n_group):
+            dy_copy(c, k).wait()
+            part += jnp.dot(
+                turned[k], gathered[k, :, columns(c)], preferred_element_type=jnp.float32
+            )
+        total[c] = part.reshape(n_dp, block, wide)
+        for k in range(1, inner):
+            for at in range(line):
+                pair_out[c, k, at] = total[c, at * inner + lax.rem(y + k, inner)].astype(
+                    jnp.bfloat16
+                )
+            pair_copy(c, k).start()
+
+    def second(c):
+        for k in range(1, inner):
+            pair_copy(c, k).wait()
+
+        def summed(at):
+            value = total[c, at * inner + y]
+            for k in range(1, inner):
+                value += pair_in[c, k, at].astype(jnp.float32)
+            return value
+
+        for j in range(1, line):
+            line_out[c, j] = summed(lax.rem(z + j, line)).astype(jnp.bfloat16)
+            line_copy(c, j).start()
+        kept[c] = summed(z)
+
+    def third(c):
+        value = kept[c]
+        for j in range(1, line):
+            line_copy(c, j).wait()
+            value += line_in[c, j].astype(jnp.float32)
+        out[:, columns(c)] = value
+
+    for c in range(chunks):
+        first(c)
+        if c:
+            second(c - 1)
+    second(chunks - 1)
+    for c in range(chunks):
+        third(c)
+
+
+def reduce_head(dy, feats, n_dp, n_group, block):
+    inner = 2 if n_dp % 2 == 0 else 1
+    line = n_dp // inner
+    tokens, emb = dy.shape
+    depth = feats.shape[2]
+    chunks = max(1, emb // 256)
+    wide = emb // chunks
+    bf16 = lambda *shape: pltpu.VMEM(shape, jnp.bfloat16)
+    f32 = lambda *shape: pltpu.VMEM(shape, jnp.float32)
+    sems = lambda *shape: pltpu.SemaphoreType.DMA(shape)
+    return pl.pallas_call(
+        functools.partial(reduce_kernel, n_dp, n_group, inner, chunks),
+        out_shape=jax.ShapeDtypeStruct((block, emb), jnp.float32),
+        in_specs=[VMEM] * 2,
+        out_specs=VMEM,
+        scratch_shapes=[
+            bf16(n_group, depth, tokens),
+            bf16(n_group, tokens, emb),
+            f32(chunks, n_dp, block, wide),
+            bf16(chunks, inner, line, block, wide),
+            bf16(chunks, inner, line, block, wide),
+            bf16(chunks, line, block, wide),
+            bf16(chunks, line, block, wide),
+            f32(chunks, block, wide),
+            sems(chunks, n_group), sems(chunks, n_group),
+            sems(chunks, inner), sems(chunks, inner),
+            sems(chunks, line), sems(chunks, line),
+        ],
+        compiler_params=pltpu.CompilerParams(has_side_effects=True),
+        name="reduce",
+    )(dy, feats)
+
+
 def dot_nt(a, b):
     return lax.dot_general(a, b, (((1,), (1,)), ((), ())), preferred_element_type=jnp.float32)
 
@@ -100,8 +361,6 @@
 
     feats = jnp.stack([query_feats, passage_feats]).reshape(2, rows, n_dp, n_group, block)
     feats = feats.transpose(3, 0, 1, 2, 4).reshape(n_group, 2 * rows, n_dp * block)
-    feats = lax.all_to_all(feats, "group", split_axis=0, concat_axis=0, tiled=True)
-    feats = feats.reshape(n_group * 2 * rows, n_dp * block)
 
     proj_query = jnp.dot(query_feats, head, preferred_element_type=jnp.float32).astype(jnp.bfloat16)
     proj_pass = jnp.dot(passage_feats, head, preferred_element_type=jnp.float32).astype(
@@ -118,10 +377,12 @@
 
     query, quant_query, inv_query = quantize(proj_query, low_bound, high_bound)
     passage, quant_pass, inv_pass = quantize(proj_pass, low_bound, high_bound)
-    batch_pass = lax.all_gather(passage, "group", axis=0, tiled=True)
-    dp_pass = lax.all_gather(passage, "dp", axis=0, tiled=True)
-    batch_query = lax.all_gather(query, "group", axis=0, tiled=True)
-    dp_query = lax.all_gather(query, "dp", axis=0, tiled=True)
+    batch_pass, dp_pass, batch_query, dp_query, feats = gather_all(
+        passage, query, feats, n_dp, n_group
+    )
+    batch_pass, dp_pass, batch_query, dp_query = (
+        x.reshape(-1, emb) for x in (batch_pass, dp_pass, batch_query, dp_query)
+    )
 
     named = (neg_ids // (n_group * rows)) * rows + neg_ids % rows
     places = jnp.arange(n_dp * rows, dtype=jnp.int32)[None, :]
@@ -161,10 +422,8 @@
     pass_grad = dot_tn(batch_arrived, batch_query) / scaling_divisor + dot_tn(chosen, hard_grad)
     dy_pass = norm_back(pass_grad, quant_pass, inv_pass)
 
-    dy = lax.all_gather(jnp.concatenate([dy_query, dy_pass]), "group", axis=0, tiled=True)
-    partial = dot_tn(feats, dy).astype(jnp.bfloat16).reshape(n_dp, block, emb)
-    shares = lax.all_to_all(partial, "dp", split_axis=0, concat_axis=0, tiled=True)
-    head_grad = jnp.sum(shares.astype(jnp.float32), axis=0)
+    dy = jnp.concatenate([dy_query, dy_pass])
+    head_grad = reduce_head(dy, feats, n_dp, n_group, block)
     return (head_grad, query_loss)
 
 

time: 299 us -> 184 us (0.62)
  waiting for transfers between devices: 114 us -> 8 us
  Pallas kernels: 18 us -> 116 us
  blocking collectives: 92.9 us -> 0 us
  between operations: 14 us -> 0.92 us
  matrix products: 28.1 us -> 21 us
  local copies, waits for them, and re-layouts: 5.4 us -> 11.6 us
    all_gather x5 -> x0, waiting for transfers between devices: 101 us -> none  [the longest x1 49.9 us: body(): dp_pass = lax.all_gather(passage, 'dp', axis=0, tiled=True)]
    pallas_call x0 -> x2, Pallas kernels: none -> 98.3 us  [the longest x1 51.7 us: gather_all(): pl.pallas_call(functools.partial(gather_kernel, n_dp, n_group, inner), ou...]
    all_to_all x2 -> x0, blocking collectives: 92.9 us -> none  [the longest x1 53.6 us: body(): lax.all_to_all(partial, 'dp', split_axis=0, concat_axis=0, tiled=True)]
    dot_general x3 -> x2, matrix products: 8.91 us -> 4.63 us  [dot_tn(): lax.dot_general(a, b, (((0,), (0,)), ((), ())), preferred_element_type=jn...]
    dot_general x1, matrix products: 5.13 us -> 1.36 us  [body(): jnp.dot(passage_feats, head, preferred_element_type=jnp.float32)]
    dot_general x1, matrix products: 1.36 us -> 4.81 us  [body(): jnp.dot(query_feats, head, preferred_element_type=jnp.float32)]
    all_to_all x1, waiting for transfers between devices: 10.2 us -> 6.96 us  [body(): lax.all_to_all(hard_weight, 'dp', split_axis=1, concat_axis=0, tiled=True)]
  transfers between devices with their start and end apart: 7 -> 2, of which waited for: 5 -> 2; matrix products, arithmetic and copies ran while one was open for 6% -> 3% of each run, Pallas kernels for 0% -> 0%
where the time goes in v2:
time: 184 us; the launch traced here: 183 us
  Pallas kernels  116 us (63%)
  matrix products  21 us (11%)
  other arithmetic  17.1 us (9%)
  local copies, waits for them, and re-layouts  11.6 us (6%)
  starting transfers between devices  8.14 us (4%)
  waiting for transfers between devices  8 us (4%)
    pallas_call x1, Pallas kernels, gather_all(): pl.pallas_call(functools.partial(gather_kernel, n_dp, n_group, inner), ou...  51.7 us
    pallas_call x1, Pallas kernels, reduce_head(): pl.pallas_call(functools.partial(reduce_kernel, n_dp, n_group, inner, chu...  46.5 us
    pallas_call x1, Pallas kernels, all_bounds(): pl.pallas_call(functools.partial(bounds_kernel, n_dp, n_group), out_shape...  18 us
    all_to_all x1, waiting for transfers between devices, body(): lax.all_to_all(hard_weight, 'dp', split_axis=1, concat_axis=0, tiled=True)  6.96 us
    dot_general x1, matrix products, body(): jnp.dot(query_feats, head, preferred_element_type=jnp.float32)  4.81 us
    all_to_all x1, starting transfers between devices, body(): lax.all_to_all(hard_weight, 'dp', split_axis=1, concat_axis=0, tiled=True)  4.64 us
    dot_general x2, matrix products, dot_tn(): lax.dot_general(a, b, (((0,), (0,)), ((), ())), preferred_element_type=jn...  4.63 us
    dot_general x2, matrix products, dot_nt(): lax.dot_general(a, b, (((1,), (1,)), ((), ())), preferred_element_type=jn...  4.56 us
  transfers between devices with their start and end apart: 2, of which 2 were waited for; matrix products, arithmetic and copies ran while one was open for 3% of the time, Pallas kernels for 0%

profile of v2, /device:TPU:0, one launch (start us, length us, event | category | flops | bytes accessed | tf_op | source)
XLA Modules:
  0.0 183.1 jit_solution(1169239469733459485)
XLA Ops:
  0.6 2.7 %stack.15 = bf16[1,128,8,4,128]{4,3,2,1,0:T(4,128)(2,1)} reshape(bf16[128,4096]{1,0:T(8,128)(2,1)} %param.4) | data formatting | bytes 2097152 | tf_op jit(solution)/shard_map/stack | solution.py:362
  3.3 4.8 %fusion.26 = (bf16[1024]{0:T(1024)(128)(2,1)S(1)}, bf16[1024]{0:T(1024)(128)(2,1)S(1)}, bf16[128,1024]{1,0:T(8,128)(2,1)S(1)}) fusion(bf16[128,4096]{1,0:T(8,128)(2,1)S(1)} %copy-done.1, bf16[4096,1024]{1,0:T(8,128)(2,1)} %param.6), kind=kOutput, calls=%fused_computation.86 | convolution fusion | flops 1074132992 | bytes 9703424 | tf_op jit(solution)/shard_map/dot_general | solution.py:365
  8.1 0.9 copy-done
  9.3 1.4 fusion.25
  10.7 1.6 stack.16
  12.9 18.0 %bounds.1 = f32[2,1024]{1,0:T(2,128)} custom-call(f32[2,1024]{1,0:T(2,128)} %pad_maximum_fusion.1.own), custom_call_target="tpu_custom_call" | custom-call | tf_op jit(solution)/shard_map/bounds/pallas_call | solution.py:65
  32.2 2.3 %reshape.116.feats = bf16[4,256,1024]{2,1,0:T(8,128)(2,1)} reshape(bf16[4,2,128,8,128]{4,3,2,1,0:T(8,128)(2,1)S(1)} %maximum_bitcast_fusion) | data formatting | bytes 4194304 | tf_op jit(solution)/shard_map/reshape | solution.py:363
  34.6 4.1 %multiply_reduce_fusion.3 = (f32[128]{0:T(128)S(1)}, f32[128]{0:T(128)S(1)}) fusion(bf16[128,1024]{1,0:T(8,128)(2,1)S(1)} %get-tuple-element.43, f32[1024]{0:T(1024)S(1)} %bitcast.63, f32[1024]{0:T(1024)S(1)} %bitcast.59, bf16[128,1024]{1,0:T(8,128)(2,1)S(1)} %get-tuple-element.44), kind=kLoop, calls=%fused_computation.34 | loop fusion | flops 2621184 | bytes 533504 | tf_op jit(solution)/shard_map/reduce_sum | solution.py:24
  39.3 4.5 %multiply_convert_fusion.5 = (bf16[128,1024]{1,0:T(8,128)(2,1)}, bf16[128,1024]{1,0:T(8,128)(2,1)}) fusion(f32[128]{0:T(128)S(1)} %get-tuple-element.49, bf16[128,1024]{1,0:T(8,128)(2,1)S(1)} %get-tuple-element.43, f32[1024]{0:T(1024)S(1)} %bitcast.64, f32[1024]{0:T(1024)S(1)} %bitcast.60, f32[128]{0:T(128)S(1)} %get-tuple-element.42, ...), kind=kLoop, calls=%fused_computation.33 | loop fusion | flops 2621440 | bytes 1057792 | tf_op jit(solution)/shard_map/convert_element_type | solution.py:25
  43.8 51.7 %gather.1 = (bf16[4,128,1024]{2,1,0:T(8,128)(2,1)}, bf16[8,128,1024]{2,1,0:T(8,128)(2,1)}, bf16[4,128,1024]{2,1,0:T(8,128)(2,1)}, bf16[8,128,1024]{2,1,0:T(8,128)(2,1)}, bf16[4,256,1024]{2,1,0:T(8,128)(2,1)}) custom-call(bf16[128,1024]{1,0:T(8,128)(2,1)} %get-tuple-element.25.passage, bf16[128,1024]{1,0:T(8,128)(2,1)} %get-tuple-element.24.query, ...), custom_call_target="tpu_custom_call" | custom-call | tf_op jit(solution)/shard_map/gather/pallas_call | solution.py:207
  95.5 1.8 exponential_reduce_fusion
  97.3 2.7 %fusion.27 = (f32[128]{0:T(128)S(1)}, f32[128,1024]{1,0:T(8,128)S(1)}) fusion(bf16[128,1024]{1,0:T(8,128)(2,1)S(1)} %copy-done.5, bf16[1024,1024]{1,0:T(8,128)(2,1)} %bitcast.54, s32[128]{0:T(128)S(1)} %get-tuple-element.29, s32[128]{0:T(128)S(1)} %get-tuple-element.30, s32[128]{0:T(128)S(1)} %get-tuple-element.31, s32[128]{0:T(128)S(1)} %get-tuple-element.32, ...), kind=kOutput, calls=%fused_computation.87 | convolution fusion | flops 270532480 | bytes 2887680 | tf_op jit(solution)/shard_map/dot_general | solution.py:346
  100.8 0.8 copy.11
  101.6 4.6 %all-to-all-start.1 = ((bf16[128,8,128]{0,2,1:T(8,128)(2,1)}), bf16[128,8,128]{0,2,1:T(8,128)(2,1)S(1)}, u32[]{:S(2)}, u32[]{:S(2)}) async-start(bf16[128,8,128]{0,2,1:T(8,128)(2,1)} %bitcast.58), calls=%async_computation.1 | async-start | bytes 524288 | tf_op jit(solution)/shard_map/all_to_all | solution.py:411
  107.8 1.2 fusion.28
  109.1 7.0 %all-to-all-done.1 = bf16[128,8,128]{0,2,1:T(8,128)(2,1)S(1)} async-done(((bf16[128,8,128]{0,2,1:T(8,128)(2,1)}), bf16[128,8,128]{0,2,1:T(8,128)(2,1)S(1)}, u32[]{:S(2)}, u32[]{:S(2)}) %all-to-all-start.1) | async-done | bytes 262176 | tf_op jit(solution)/shard_map/all_to_all | solution.py:411
  116.0 3.5 %all-to-all-start = ((bf16[128,4,128]{0,2,1:T(8,128)(2,1)}), bf16[128,4,128]{0,2,1:T(8,128)(2,1)S(1)}, u32[]{:S(2)}, u32[]{:S(2)}) async-start(bf16[128,4,128]{0,2,1:T(8,128)(2,1)} %bitcast.14), calls=%async_computation | async-start | bytes 262144 | tf_op jit(solution)/shard_map/all_to_all | solution.py:410
  119.6 3.3 %fusion.3 = f32[128,1024]{1,0:T(8,128)} fusion(bf16[8,128,1024]{2,1,0:T(8,128)(2,1)} %get-tuple-element.10, f32[8,128]{1,0:T(8,128)S(1)} %bitcast.69, bf16[128,8,128]{0,2,1:T(8,128)(2,1)S(1)} %all-to-all-done.1), kind=kOutput, calls=%fused_computation.6 | convolution fusion | flops 272760832 | bytes 2887680 | tf_op jit(solution)/shard_map/dot_general | solution.py:350
  122.9 1.0 all-to-all-done
  123.9 1.4 fusion.5
  125.4 4.4 %multiply_reduce_fusion.1 = (f32[128]{0:T(128)S(1)}, f32[128]{0:T(128)S(1)}, f32[128,1024]{1,0:T(8,128)S(1)}) fusion(bf16[128,1024]{1,0:T(8,128)(2,1)S(1)} %get-tuple-element.43, f32[1024]{0:T(1024)S(1)} %bitcast.65, f32[1024]{0:T(1024)S(1)} %bitcast.61, f32[128,1024]{1,0:T(8,128)S(1)} %fusion.5, bf16[128,1024]{1,0:T(8,128)(2,1)S(1)} %get-tuple-element.44, ...), kind=kOutput, calls=%fused_computation.21 | convolution fusion | flops 137101056 | bytes 3286016 | tf_op jit(solution)/shard_map/dot_general | solution.py:414
  129.8 4.0 %subtract_convert_fusion.1 = (bf16[128,1024]{1,0:T(8,128)(2,1)S(1)}, bf16[128,1024]{1,0:T(8,128)(2,1)S(1)}) fusion(f32[128,1024]{1,0:T(8,128)S(1)} %get-tuple-element.48, f32[128]{0:T(128)S(1)} %get-tuple-element.18, f32[128]{0:T(128)S(1)} %copy-done.13, f32[128]{0:T(128)S(1)} %copy-done.14, bf16[128,1024]{1,0:T(8,128)(2,1)S(1)} %get-tuple-element.43, ...), kind=kLoop, calls=%fused_computation.20 | loop fusion | flops 3407872 | bytes 2108416 | tf_op jit(solution)/shard_map/convert_element_type | solution.py:30
  134.7 46.5 %reduce.3 = f32[128,1024]{1,0:T(8,128)} custom-call(bf16[256,1024]{1,0:T(8,128)(2,1)} %pad_maximum_fusion.dy, bf16[4,256,1024]{2,1,0:T(8,128)(2,1)} %get-tuple-element.11.feats), custom_call_target="tpu_custom_call" | custom-call | tf_op jit(solution)/shard_map/reduce/pallas_call | solution.py:322
  181.2 1.9 %copy.13 = f32[128,1024]{1,0:T(8,128)} copy(f32[128,1024]{1,0:T(8,128)} %reduce.3) | data formatting | bytes 1048576
  (46 shorter events, 5.9 us)
Async XLA Ops:
  0.6 2.7 %copy-start.1 = (bf16[128,4096]{1,0:T(8,128)(2,1)S(1)}, bf16[128,4096]{1,0:T(8,128)(2,1)}, u32[]{:S(2)}) copy-start(bf16[128,4096]{1,0:T(8,128)(2,1)} %param.4) | copy-start | bytes 3145732
  3.3 5.8 %copy-start = (bf16[4096,1024]{1,0:T(8,128)(2,1)S(1)}, bf16[4096,1024]{1,0:T(8,128)(2,1)}, u32[]{:S(2)}) copy-start(bf16[4096,1024]{1,0:T(8,128)(2,1)} %param.6) | copy-start | bytes 25165828
  3.3 6.0 %copy-start.2 = (bf16[128,4096]{1,0:T(8,128)(2,1)S(1)}, bf16[128,4096]{1,0:T(8,128)(2,1)}, u32[]{:S(2)}) copy-start(bf16[128,4096]{1,0:T(8,128)(2,1)} %param.5) | copy-start | bytes 3145732
  10.7 21.0 %copy-start.3 = (bf16[1,128,8,4,128]{4,3,2,1,0:T(4,128)(2,1)S(1)}, bf16[1,128,8,4,128]{4,3,2,1,0:T(4,128)(2,1)}, u32[]{:S(2)}) copy-start(bf16[1,128,8,4,128]{4,3,2,1,0:T(4,128)(2,1)} %stack.15) | copy-start | bytes 3145732
  12.3 19.6 %copy-start.4 = (bf16[1,128,8,4,128]{4,3,2,1,0:T(4,128)(2,1)S(1)}, bf16[1,128,8,4,128]{4,3,2,1,0:T(4,128)(2,1)}, u32[]{:S(2)}) copy-start(bf16[1,128,8,4,128]{4,3,2,1,0:T(4,128)(2,1)} %stack.16) | copy-start | bytes 3145732
  32.2 2.4 %copy-start.10 = (s32[128,7]{0,1:T(8,128)S(1)}, s32[128,7]{0,1:T(8,128)}, u32[]{:S(2)}) copy-start(s32[128,7]{0,1:T(8,128)} %param.7) | copy-start | bytes 10756
  34.6 60.9 %copy-start.11 = (s32[128]{0:T(128)}, s32[128]{0:T(128)S(1)}, u32[]{:S(2)}) copy-start(s32[128]{0:T(128)S(1)} %iota_add_fusion) | copy-start | bytes 1540
  43.7 51.8 %copy-start.5 = (bf16[128,1024]{1,0:T(8,128)(2,1)S(1)}, bf16[128,1024]{1,0:T(8,128)(2,1)}, u32[]{:S(2)}) copy-start(bf16[128,1024]{1,0:T(8,128)(2,1)} %get-tuple-element.24.query) | copy-start | bytes 786436
  100.1 7.8 %copy-start.6 = (bf16[8,128,1024]{2,1,0:T(8,128)(2,1)S(1)}, bf16[8,128,1024]{2,1,0:T(8,128)(2,1)}, u32[]{:S(2)}) copy-start(bf16[8,128,1024]{2,1,0:T(8,128)(2,1)} %get-tuple-element.8) | copy-start | bytes 6291460
  101.6 14.4 %all-to-all-start.1 = ((bf16[128,8,128]{0,2,1:T(8,128)(2,1)}), bf16[128,8,128]{0,2,1:T(8,128)(2,1)S(1)}, u32[]{:S(2)}, u32[]{:S(2)}) async-start(bf16[128,8,128]{0,2,1:T(8,128)(2,1)} %bitcast.58), calls=%async_computation.1 | async-start | bytes 524288 | tf_op jit(solution)/shard_map/all_to_all | solution.py:411
  116.0 7.9 %all-to-all-start = ((bf16[128,4,128]{0,2,1:T(8,128)(2,1)}), bf16[128,4,128]{0,2,1:T(8,128)(2,1)S(1)}, u32[]{:S(2)}, u32[]{:S(2)}) async-start(bf16[128,4,128]{0,2,1:T(8,128)(2,1)} %bitcast.14), calls=%async_computation | async-start | bytes 262144 | tf_op jit(solution)/shard_map/all_to_all | solution.py:410
  119.6 4.3 %copy-start.8 = (bf16[4,128,1024]{2,1,0:T(8,128)(2,1)S(1)}, bf16[4,128,1024]{2,1,0:T(8,128)(2,1)}, u32[]{:S(2)}) copy-start(bf16[4,128,1024]{2,1,0:T(8,128)(2,1)} %get-tuple-element.9) | copy-start | bytes 3145732
  122.9 2.4 %copy-start.7 = (bf16[4,128,1024]{2,1,0:T(8,128)(2,1)S(1)}, bf16[4,128,1024]{2,1,0:T(8,128)(2,1)}, u32[]{:S(2)}) copy-start(bf16[4,128,1024]{2,1,0:T(8,128)(2,1)} %get-tuple-element.7) | copy-start | bytes 3145732
  122.9 2.4 %copy-start.9 = (f32[128,1024]{1,0:T(8,128)S(1)}, f32[128,1024]{1,0:T(8,128)}, u32[]{:S(2)}) copy-start(f32[128,1024]{1,0:T(8,128)} %fusion.28) | copy-start | bytes 1572868
  125.3 4.4 %copy-start.12 = (f32[128]{0:T(128)S(1)}, f32[128]{0:T(128)}, u32[]{:S(2)}) copy-start(f32[128]{0:T(128)} %get-tuple-element.41) | copy-start | bytes 1540
  125.3 4.4 %copy-start.13 = (f32[128]{0:T(128)S(1)}, f32[128]{0:T(128)}, u32[]{:S(2)}) copy-start(f32[128]{0:T(128)} %get-tuple-element.50) | copy-start | bytes 1540
  125.3 4.4 %copy-start.14 = (f32[128]{0:T(128)S(1)}, f32[128]{0:T(128)}, u32[]{:S(2)}) copy-start(f32[128]{0:T(128)} %get-tuple-element.51) | copy-start | bytes 1540

commit v3 on v1

v3 whole, which is shorter than its diff:
```python
import functools
import math

import jax
import jax.numpy as jnp
from jax import lax
from jax.experimental import pallas as pl
from jax.experimental.pallas import tpu as pltpu
from jax.sharding import PartitionSpec as P

scaling_divisor = 0.05
levels = 15.0
epsilon = 1e-06
MESH = pl.DeviceIdType.MESH
VMEM = pl.BlockSpec(memory_space=pltpu.VMEM)


def quantize(projected, low, stride, inv_stride):
    level = (projected.astype(jnp.float32) - low) * inv_stride
    turn = level - jnp.floor(level + 0.5)
    quarter = 0.25 - jnp.abs(jnp.abs(turn) - 0.25)
    angle = jnp.where(turn < 0, -quarter, quarter) * (2.0 * math.pi)
    square = angle * angle
    series = -1.0 / math.factorial(11)
    for order in (9, 7, 5, 3, 1):
        series = (-1.0) ** (order // 2) / math.factorial(order) + square * series
    return low + stride * (level - angle * series * (1.0 / (2.0 * math.pi)))


def norm_back(cotangent, quantized, inverse):
    inner_prod = jnp.sum(quantized * cotangent, axis=-1, keepdims=True)
    return (inverse * cotangent - quantized * (inverse**3 * inner_prod)).astype(jnp.bfloat16)


def dot_nn(a, b):
    return jnp.dot(a, b, preferred_element_type=jnp.float32)


def dot_nt(a, b):
    return lax.dot_general(a, b, (((1,), (1,)), ((), ())), preferred_element_type=jnp.float32)


def dot_tn(a, b):
    return lax.dot_general(a, b, (((0,), (0,)), ((), ())), preferred_element_type=jnp.float32)


def remote(src, dst, send, recv, device):
    return pltpu.make_async_remote_copy(
        src_ref=src,
        dst_ref=dst,
        send_sem=send,
        recv_sem=recv,
        device_id=device,
        device_id_type=MESH,
    )


def step_kernel(
    n_dp, n_group, inner, chunks,
    proj_query, proj_pass, stats, query_feats, pass_feats, named, out, loss,
    stats_group, stats_dp, stats_mid,
    emb_query, emb_pass, quant_query, quant_pass, inv_query, inv_pass,
    batch_query, batch_pass, dp_query, dp_pass, hard_exp,
    batch_out, batch_in, hard_out, hard_in,
    feats, turned, dy, gathered, total, pair_out, pair_in, line_out, line_in, kept,
    s_stat_g, r_stat_g, s_stat_d, r_stat_d, s_feat, r_feat,
    s_line, s_pair, r_dp, s_batch, r_batch, s_bw, r_bw, s_hw, r_hw,
    s_dy, r_dy, s_p, r_p, s_l, r_l,
):
    me_d, me_g = lax.axis_index("dp"), lax.axis_index("group")
    line = n_dp // inner
    z, y = me_d // inner, lax.rem(me_d, inner)
    rows, emb = proj_query.shape
    wide = emb // chunks
    block = out.shape[0]
    columns = lambda c: pl.ds(c * wide, wide)
    group_at = lambda k: lax.rem(me_g + k, n_group)
    group_from = lambda k: lax.rem(me_g + n_group - k, n_group)
    dp_at = lambda k: lax.rem(me_d + k, n_dp)
    dp_from = lambda k: lax.rem(me_d + n_dp - k, n_dp)

    def feat_copy(i, k):
        src = (query_feats, pass_feats)[i]
        return remote(
            src.at[group_at(k)], feats.at[i, k], s_feat.at[i, k], r_feat.at[i, k], (me_d, group_at(k))
        )

    def largest(src, landing, send, recv, count, target):
        copies = []
        for k in range(1, count):
            copies.append(remote(src, landing.at[k], send.at[k], recv.at[k], target(k)))
            copies[-1].start()
        value = src[...]
        for k in range(1, count):
            copies[k - 1].wait()
            value = jnp.maximum(value, landing[k])
        return value

    stats_mid[...] = largest(
        stats, stats_group, s_stat_g, r_stat_g, n_group, lambda k: (me_d, group_at(k))
    )
    for i in range(2):
        for k in range(1, n_group):
            feat_copy(i, k).start()
    bounds = largest(stats_mid, stats_dp, s_stat_d, r_stat_d, n_dp, lambda k: (dp_at(k), me_g))
    high, low = bounds[0:1], -bounds[1:2]
    stride = (high - low) / levels
    inv_stride = 1.0 / stride

    items = ((emb_pass, batch_pass, dp_pass), (emb_query, batch_query, dp_query))

    def slot_copy(i, source, src, send, target):
        return remote(src, items[i][2].at[source], send, r_dp.at[i, source], (target, me_g))

    def forwards(i, at, src, rightward, leftward):
        source = at * inner + y
        copies = []
        if rightward:
            copies.append((z < line - 1, slot_copy(i, source, src, s_line.at[i, 0, at], dp_at(inner))))
        if leftward:
            copies.append((z > 0, slot_copy(i, source, src, s_line.at[i, 1, at], dp_from(inner))))
        for k in range(1, inner):
            target = z * inner + lax.rem(y + k, inner)
            copies.append((None, slot_copy(i, source, src, s_pair.at[i, k, at], target)))
        return copies

    def each(copies, act):
        for condition, copy in copies:
            if condition is None:
                act(copy)
            else:
                pl.when(condition)(functools.partial(act, copy))

    def start(copy):
        copy.start()

    def wait_send(copy):
        copy.wait_send()

    def batch_copy(i, k):
        return remote(
            items[i][0], items[i][1].at[k], s_batch.at[i, k], r_batch.at[i, k], (me_d, group_at(k))
        )

    def start_own(i):
        each(forwards(i, z, items[i][0], True, True), start)
        for k in range(1, n_group):
            batch_copy(i, k).start()

    def relay(i, s):
        for at, inside, onward in ((z - s, z >= s, True), (z + s, z + s < line, False)):

            @pl.when(inside)
            def _(at=at, onward=onward):
                source = at * inner + y
                arrived = items[i][2].at[source]
                slot_copy(i, source, arrived, s_line.at[i, 0, at], me_d).wait_recv()
                each(forwards(i, at, arrived, onward, not onward), start)

    def wait_pairs(i):
        for k in range(1, inner):
            for at in range(line):
                source = at * inner + lax.rem(y + k, inner)
                arrived = items[i][2].at[source]
                slot_copy(i, source, arrived, s_pair.at[i, k, at], me_d).wait_recv()

    def wait_all_sent(i):
        each(forwards(i, z, items[i][0], True, True), wait_send)
        for s in range(1, line):
            for at, inside, onward in ((z - s, z >= s, True), (z + s, z + s < line, False)):

                @pl.when(inside)
                def _(at=at, onward=onward):
                    arrived = items[i][2].at[at * inner + y]
                    each(forwards(i, at, arrived, onward, not onward), wait_send)

    def embed(projected, quant, inverse, emb_ref):
        value = quantize(projected[...], low, stride, inv_stride)
        inv = lax.rsqrt(jnp.sum(value * value, axis=-1, keepdims=True) + epsilon)
        quant[...] = value
        inverse[...] = inv
        emb_ref[...] = (value * inv).astype(jnp.bfloat16)

    embed(proj_pass, quant_pass, inv_pass, emb_pass)
    start_own(0)
    embed(proj_query, quant_query, inv_query, emb_query)
    for s in range(1, line):
        relay(0, s)
    start_own(1)

    for i in range(2):
        for k in range(1, n_group):
            feat_copy(i, k).wait()
        lanes = pl.ds(i * rows, rows)
        turned[0, :, lanes] = (query_feats, pass_feats)[i][me_g].T
        for k in range(1, n_group):
            turned[k, :, lanes] = feats[i, k].T

    for k in range(1, n_group):
        batch_copy(0, k).wait()
    wait_pairs(0)
    if line > 1:
        relay(1, 1)

    def over_dp(step, value):
        if n_dp > 16:
            return lax.fori_loop(1, n_dp, step, value)
        for k in range(1, n_dp):
            value = step(k, value)
        return value

    query = emb_query[...]
    eye = (
        lax.broadcasted_iota(jnp.int32, (rows, rows), 0)
        == lax.broadcasted_iota(jnp.int32, (rows, rows), 1)
    ).astype(jnp.float32)
    place = lax.broadcasted_iota(jnp.int32, (rows, rows), 1)
    batch_block = lambda k: emb_pass[...] if k == 0 else batch_pass[k]
    scores = [dot_nt(query, batch_block(k)) / scaling_divisor for k in range(n_group)]
    positive = jnp.sum(scores[0] * eye, axis=1, keepdims=True)
    exp_batch = [jnp.exp(score) for score in scores]
    batch_total = sum(jnp.sum(value, axis=1, keepdims=True) for value in exp_batch)
    exp_pos = jnp.exp(positive)

    def hard_step(k, hard_sum):
        source = dp_at(k)
        score = dot_nt(query, dp_pass[source]) / scaling_divisor
        here = named[:, 0:1] == place + source * rows
        for n in range(1, named.shape[1]):
            here = here | (named[:, n : n + 1] == place + source * rows)
        value = jnp.where(here, jnp.exp(score), 0.0)
        hard_exp[k] = value
        return hard_sum + value

    hard_sum = over_dp(hard_step, jnp.zeros((rows, rows), jnp.float32))
    hard_total = exp_pos + jnp.sum(hard_sum, axis=1, keepdims=True)
    loss[...] = jnp.log(batch_total) - positive + jnp.log(hard_total) - positive

    def weight_copy(k):
        return remote(
            batch_out.at[k], batch_in.at[k], s_bw.at[k], r_bw.at[k], (me_d, group_from(k))
        )

    def hard_copy(k):
        return remote(hard_out.at[k], hard_in.at[k], s_hw.at[k], r_hw.at[k], (dp_at(k), me_g))

    for k in range(n_group):
        weight = exp_batch[k] / batch_total
        if k == 0:
            weight = weight - eye * (2.0 - exp_pos / hard_total)
        batch_out[k] = weight.astype(jnp.bfloat16)
        if k:
            weight_copy(k).start()

    def hard_send(k, nothing):
        hard_out[k] = (hard_exp[k] / hard_total).astype(jnp.bfloat16)
        hard_copy(k).start()
        return nothing

    over_dp(hard_send, 0)
    if line > 2:
        relay(1, 2)

    grad = dot_nn(batch_out[0], emb_pass[...])
    for k in range(1, n_group):
        grad += dot_nn(batch_out[k], batch_pass[k])
    grad = over_dp(lambda k, value: value + dot_nn(hard_out[k], dp_pass[dp_at(k)]), grad)
    dy[0] = norm_back(grad / scaling_divisor, quant_query[...], inv_query[...])

    def dy_copy(i, c, k):
        return remote(
            dy.at[i, :, columns(c)], gathered.at[k, pl.ds(i * rows, rows), columns(c)],
            s_dy.at[i, c, k], r_dy.at[i, c, k], (me_d, group_at(k)),
        )

    for c in range(chunks):
        for k in range(1, n_group):
            dy_copy(0, c, k).start()
    for s in range(3, line):
        relay(1, s)

    for k in range(1, n_group):
        batch_copy(1, k).wait()
        weight_copy(k).wait()
    grad = dot_tn(batch_out[0], emb_query[...])
    for k in range(1, n_group):
        grad += dot_tn(batch_in[k], batch_query[n_group - k])
    grad = grad / scaling_divisor
    wait_pairs(1)

    def hard_back(k, value):
        hard_copy(k).wait()
        weight = hard_in[k]
        one = jnp.sum(weight.astype(jnp.float32), axis=1, keepdims=True)
        hard = (one * dp_query[dp_from(k)].astype(jnp.float32) * (1.0 / scaling_divisor)).astype(
            jnp.bfloat16
        )
        chosen = jnp.where(weight.astype(jnp.float32) != 0, 1.0, 0.0).astype(jnp.bfloat16)
        return value + dot_tn(chosen, hard)

    dy[1] = norm_back(over_dp(hard_back, grad), quant_pass[...], inv_pass[...])
    for c in range(chunks):
        for k in range(1, n_group):
            dy_copy(1, c, k).start()

    def pair_copy(c, k):
        target = z * inner + lax.rem(y + k, inner)
        return remote(
            pair_out.at[c, k - 1], pair_in.at[c, k - 1], s_p.at[c, k], r_p.at[c, k], (target, me_g)
        )

    def line_copy(c, j):
        target = lax.rem(z + j, line) * inner + y
        return remote(
            line_out.at[c, j], line_in.at[c, j], s_l.at[c, j], r_l.at[c, j], (target, me_g)
        )

    def first(c):
        part = dot_nn(turned[0, :, 0:rows], dy[0, :, columns(c)])
        part += dot_nn(turned[0, :, rows:], dy[1, :, columns(c)])
        for k in range(1, n_group):
            dy_copy(0, c, k).wait()
            dy_copy(1, c, k).wait()
            part += dot_nn(turned[k], gathered[k, :, columns(c)])
        total[c] = part.reshape(n_dp, block, wide)
        for k in range(1, inner):
            for at in range(line):
                pair_out[c, k - 1, at] = total[c, at * inner + lax.rem(y + k, inner)].astype(
                    jnp.bfloat16
                )
            pair_copy(c, k).start()

    def second(c):
        for k in range(1, inner):
            pair_copy(c, k).wait()

        def summed(at):
            value = total[c, at * inner + y]
            for k in range(1, inner):
                value += pair_in[c, k - 1, at].astype(jnp.float32)
            return value

        for j in range(1, line):
            line_out[c, j] = summed(lax.rem(z + j, line)).astype(jnp.bfloat16)
            line_copy(c, j).start()
        kept[c] = summed(z)

    def third(c):
        value = kept[c]
        for j in range(1, line):
            line_copy(c, j).wait()
            value += line_in[c, j].astype(jnp.float32)
        out[:, columns(c)] = value

    for c in range(chunks):
        first(c)
        if c:
            second(c - 1)
    second(chunks - 1)
    for i in range(2):
        wait_all_sent(i)
    for c in range(chunks):
        third(c)


def whole_step(proj_query, proj_pass, stats, query_feats, pass_feats, named, n_dp, n_group, block):
    inner = 2 if n_dp % 2 == 0 else 1
    line = n_dp // inner
    rows, emb = proj_query.shape
    depth = query_feats.shape[2]
    chunks = max(1, emb // 256)
    wide = emb // chunks
    bf16 = lambda *shape: pltpu.VMEM(shape, jnp.bfloat16)
    f32 = lambda *shape: pltpu.VMEM(shape, jnp.float32)
    sems = lambda *shape: [pltpu.SemaphoreType.DMA(shape)]
    pairs = lambda *shape: sems(*shape) * 2
    return pl.pallas_call(
        functools.partial(step_kernel, n_dp, n_group, inner, chunks),
        out_shape=(
            jax.ShapeDtypeStruct((block, emb), jnp.float32),
            jax.ShapeDtypeStruct((rows, 1), jnp.float32),
        ),
        in_specs=[VMEM] * 6,
        out_specs=(VMEM, VMEM),
        scratch_shapes=[
            f32(n_group, 2, emb), f32(n_dp, 2, emb), f32(2, emb),
            bf16(rows, emb), bf16(rows, emb), f32(rows, emb), f32(rows, emb), f32(rows, 1), f32(rows, 1),
            bf16(n_group, rows, emb), bf16(n_group, rows, emb), bf16(n_dp, rows, emb), bf16(n_dp, rows, emb),
            f32(n_dp, rows, rows),
            bf16(n_group, rows, rows), bf16(n_group, rows, rows), bf16(n_dp, rows, rows), bf16(n_dp, rows, rows),
            bf16(2, n_group, rows, depth), bf16(n_group, depth, 2 * rows), bf16(2, rows, emb),
            bf16(n_group, 2 * rows, emb),
            f32(chunks, n_dp, block, wide),
            bf16(chunks, max(1, inner - 1), line, block, wide),
            bf16(chunks, max(1, inner - 1), line, block, wide),
            bf16(chunks, line, block, wide), bf16(chunks, line, block, wide),
            f32(chunks, block, wide),
        ]
        + pairs(n_group) + pairs(n_dp) + pairs(2, n_group)
        + sems(2, 2, line) + sems(2, inner, line) + sems(2, n_dp) + pairs(2, n_group)
        + pairs(n_group) + pairs(n_dp)
        + pairs(2, chunks, n_group) + pairs(chunks, inner) + pairs(chunks, line),
        compiler_params=pltpu.CompilerParams(has_side_effects=True, vmem_limit_bytes=67043328),
        name="step",
    )(proj_query, proj_pass, stats, query_feats, pass_feats, named)


def body(query_feats, passage_feats, head, neg_ids):
    rows, width = query_feats.shape
    emb = head.shape[1]
    n_dp = lax.axis_size("dp")
    n_group = lax.axis_size("group")
    block = width // (n_dp * n_group)

    def cut(feats):
        feats = feats.reshape(rows, n_dp, n_group, block)
        return feats.transpose(2, 0, 1, 3).reshape(n_group, rows, n_dp * block)

    proj_query = jnp.dot(query_feats, head, preferred_element_type=jnp.float32).astype(jnp.bfloat16)
    proj_pass = jnp.dot(passage_feats, head, preferred_element_type=jnp.float32).astype(
        jnp.bfloat16
    )
    col_high = jnp.maximum(jnp.max(proj_query, axis=0), jnp.max(proj_pass, axis=0)).astype(
        jnp.float32
    )
    col_low = jnp.minimum(jnp.min(proj_query, axis=0), jnp.min(proj_pass, axis=0)).astype(
        jnp.float32
    )
    named = (neg_ids // (n_group * rows)) * rows + neg_ids % rows
    head_grad, query_loss = whole_step(
        proj_query, proj_pass, jnp.stack([col_high, -col_low]), cut(query_feats),
        cut(passage_feats), named, n_dp, n_group, block,
    )
    return (head_grad, query_loss.reshape(rows))


def solution(mesh):
    return jax.shard_map(
        body,
        mesh=mesh,
        in_specs=(
            P(("dp", "group"), None),
            P(("dp", "group"), None),
            P(),
            P(("dp", "group"), None),
        ),
        out_specs=(P(("dp", "group"), None), P(("dp", "group"))),
        check_vma=False,
    )
```

time: 299 us -> 131 us (0.44)
  waiting for transfers between devices: 114 us -> 0 us
  Pallas kernels: 18 us -> 112 us
  blocking collectives: 92.9 us -> 0 us
  matrix products: 28.1 us -> 7.88 us
  other arithmetic: 18.6 us -> 2.75 us
  between operations: 14 us -> 0.7 us
  starting transfers between devices: 7.11 us -> 0 us
    all_gather x5 -> x0, waiting for transfers between devices: 101 us -> none  [the longest x1 49.9 us: body(): dp_pass = lax.all_gather(passage, 'dp', axis=0, tiled=True)]
    pallas_call x1, Pallas kernels: 18 us -> 112 us  [whole_step(): pl.pallas_call(functools.partial(step_kernel, n_dp, n_group, inner, chunk...]
    all_to_all x2 -> x0, blocking collectives: 92.9 us -> none  [the longest x1 53.6 us: body(): lax.all_to_all(partial, 'dp', split_axis=0, concat_axis=0, tiled=True)]
    dot_general x7 -> x0, matrix products: 21.7 us -> none  [the longest x3 8.91 us: dot_tn(): lax.dot_general(a, b, (((0,), (0,)), ((), ())), preferred_element_type=jn...]
    all_to_all x2 -> x0, waiting for transfers between devices: 10.2 us -> none  [the longest x1 10.2 us: body(): lax.all_to_all(hard_weight, 'dp', split_axis=1, concat_axis=0, tiled=True)]
    convert_element_type x2 -> x0, other arithmetic: 8.53 us -> none  [the longest x1 4.48 us: quantize(): return ((quantized * inverse).astype(jnp.bfloat16), quantized, inverse)]
    all_to_all x2 -> x0, starting transfers between devices: 6.74 us -> none  [the longest x1 3.41 us: body(): lax.all_to_all(hard_weight, 'dp', split_axis=1, concat_axis=0, tiled=True)]
    reduce_sum x3 -> x0, other arithmetic: 5.36 us -> none  [the longest x1 4.07 us: quantize(): jnp.sum(quantized * quantized, axis=-1, keepdims=True) + epsilon]
  transfers between devices with their start and end apart: 7 -> 0, of which waited for: 5 -> 0; matrix products, arithmetic and copies ran while one was open for 6% -> 0% of each run, Pallas kernels for 0% -> 0%
where the time goes in v3:
time: 131 us; the launch traced here: 130 us
  Pallas kernels  112 us (85%)
  matrix products  7.88 us (6%)
  local copies, waits for them, and re-layouts  6.93 us (5%)
  other arithmetic  2.75 us (2%)
    pallas_call x1, Pallas kernels, whole_step(): pl.pallas_call(functools.partial(step_kernel, n_dp, n_group, inner, chunk...  112 us
    dot_general x1, matrix products, body(): jnp.dot(passage_feats, head, preferred_element_type=jnp.float32)  5.82 us

profile of v3, /device:TPU:0, one launch (start us, length us, event | category | flops | bytes accessed | tf_op | source)
XLA Modules:
  0.0 130.5 jit_solution(1829935555327416271)
XLA Ops:
  0.6 0.0 copy-start
  0.6 0.0 copy-start.1
  0.6 5.8 %fusion.5 = (bf16[1024]{0:T(1024)(128)(2,1)S(1)}, bf16[1024]{0:T(1024)(128)(2,1)S(1)}, bf16[128,1024]{1,0:T(8,128)(2,1)}) fusion(bf16[128,4096]{1,0:T(8,128)(2,1)} %param.5, bf16[4096,1024]{1,0:T(8,128)(2,1)} %param.6), kind=kOutput, calls=%fused_computation.19 | convolution fusion | flops 1074132992 | bytes 9703424 | tf_op jit(solution)/shard_map/dot_general | solution.py:420
  6.5 0.2 copy-done
  6.7 0.3 copy-done.1
  7.0 0.0 copy-start.2
  7.0 2.1 %fusion.6 = (bf16[1024]{0:T(1024)(128)(2,1)S(1)}, bf16[1024]{0:T(1024)(128)(2,1)S(1)}, bf16[128,1024]{1,0:T(8,128)(2,1)}) fusion(bf16[128,4096]{1,0:T(8,128)(2,1)S(1)} %copy-done.1, bf16[4096,1024]{1,0:T(8,128)(2,1)S(1)} %copy-done), kind=kOutput, calls=%fused_computation.20 | convolution fusion | flops 1074132992 | bytes 9703424 | tf_op jit(solution)/shard_map/dot_general | solution.py:419
  9.1 0.0 copy-start.3
  9.1 0.6 pad_maximum_fusion.stats
  9.7 0.7 reshape.56
  10.5 0.1 copy.21
  10.6 1.3 reshape.57.query_feats
  11.9 0.0 copy-done.2
  11.9 0.8 reshape.58
  12.7 0.1 copy.20
  12.8 1.3 reshape.59.pass_feats
  14.1 0.0 copy-done.3
  14.1 0.1 copy.14
  14.2 0.7 fusion.2.named
  14.9 112.2 %step.1 = (f32[128,1024]{1,0:T(8,128)}, f32[128,1]{1,0:T(8,128)}) custom-call(bf16[128,1024]{1,0:T(8,128)(2,1)} %get-tuple-element.10.proj_query, bf16[128,1024]{1,0:T(8,128)(2,1)} %get-tuple-element.11.proj_pass, f32[2,1024]{1,0:T(2,128)} %pad_maximum_fusion.stats, bf16[4,128,1024]{2,1,0:T(8,128)(2,1)} %reshape.57.query_feats, ...), custom_call_target="tpu_custom_call" | custom-call | tf_op jit(solution)/shard_map/step/pallas_call | solution.py:377
  127.1 1.5 %reduce = f32[128]{0:T(128)} reduce(f32[128,1]{1,0:T(8,128)} %get-tuple-element.5, f32[]{:T(128)} %constant.35), dimensions={1}, to_apply=%get-tuple-element.5.reduce_sub_computation | reduce | bytes 1028 | tf_op jit(solution)/shard_map/step/pallas_call | solution.py:377
  128.6 1.9 %copy.23 = f32[128,1024]{1,0:T(8,128)} copy(f32[128,1024]{1,0:T(8,128)} %get-tuple-element.14) | data formatting | bytes 1048576
  (2 shorter events, 0.0 us)
Async XLA Ops:
  0.6 6.1 %copy-start = (bf16[4096,1024]{1,0:T(8,128)(2,1)S(1)}, bf16[4096,1024]{1,0:T(8,128)(2,1)}, u32[]{:S(2)}) copy-start(bf16[4096,1024]{1,0:T(8,128)(2,1)} %param.6) | copy-start | bytes 25165828
  0.6 6.4 %copy-start.1 = (bf16[128,4096]{1,0:T(8,128)(2,1)S(1)}, bf16[128,4096]{1,0:T(8,128)(2,1)}, u32[]{:S(2)}) copy-start(bf16[128,4096]{1,0:T(8,128)(2,1)} %param.4) | copy-start | bytes 3145732
  7.0 4.9 %copy-start.2 = (bf16[128,4096]{1,0:T(8,128)(2,1)S(1)}, bf16[128,4096]{1,0:T(8,128)(2,1)}, u32[]{:S(2)}) copy-start(bf16[128,4096]{1,0:T(8,128)(2,1)} %param.5) | copy-start | bytes 3145732
  9.1 5.0 %copy-start.3 = (s32[128,7]{0,1:T(8,128)S(1)}, s32[128,7]{0,1:T(8,128)}, u32[]{:S(2)}) copy-start(s32[128,7]{0,1:T(8,128)} %param.7) | copy-start | bytes 10756

commit v4 on v3

--- a/solution.py
+++ b/solution.py
@@ -65,7 +65,7 @@
     feats, turned, dy, gathered, total, pair_out, pair_in, line_out, line_in, kept,
     s_stat_g, r_stat_g, s_stat_d, r_stat_d, s_feat, r_feat,
     s_line, s_pair, r_dp, s_batch, r_batch, s_bw, r_bw, s_hw, r_hw,
-    s_dy, r_dy, s_p, r_p, s_l, r_l,
+    s_dy, r_dy, s_p, r_p, s_l, r_l, *staged
 ):
     me_d, me_g = lax.axis_index("dp"), lax.axis_index("group")
     line = n_dp // inner
@@ -79,8 +79,10 @@
     dp_at = lambda k: lax.rem(me_d + k, n_dp)
     dp_from = lambda k: lax.rem(me_d + n_dp - k, n_dp)
 
+    cut_feats = (staged[0].at[0], staged[0].at[1]) if staged else (query_feats, pass_feats)
+
     def feat_copy(i, k):
-        src = (query_feats, pass_feats)[i]
+        src = cut_feats[i]
         return remote(
             src.at[group_at(k)], feats.at[i, k], s_feat.at[i, k], r_feat.at[i, k], (me_d, group_at(k))
         )
@@ -95,6 +97,14 @@
             copies[k - 1].wait()
             value = jnp.maximum(value, landing[k])
         return value
+
+    if staged:
+        for i, whole in enumerate((query_feats, pass_feats)):
+            for d in range(n_dp):
+                for g in range(n_group):
+                    staged[0][i, g, :, d * block : (d + 1) * block] = whole[
+                        :, (d * n_group + g) * block : (d * n_group + g + 1) * block
+                    ]
 
     stats_mid[...] = largest(
         stats, stats_group, s_stat_g, r_stat_g, n_group, lambda k: (me_d, group_at(k))
@@ -192,7 +202,7 @@
         for k in range(1, n_group):
             feat_copy(i, k).wait()
         lanes = pl.ds(i * rows, rows)
-        turned[0, :, lanes] = (query_feats, pass_feats)[i][me_g].T
+        turned[0, :, lanes] = cut_feats[i][me_g].T
         for k in range(1, n_group):
             turned[k, :, lanes] = feats[i, k].T
 
@@ -234,7 +244,8 @@
 
     hard_sum = over_dp(hard_step, jnp.zeros((rows, rows), jnp.float32))
     hard_total = exp_pos + jnp.sum(hard_sum, axis=1, keepdims=True)
-    loss[...] = jnp.log(batch_total) - positive + jnp.log(hard_total) - positive
+    column = jnp.log(batch_total) - positive + jnp.log(hard_total) - positive
+    loss[...] = jnp.sum(column * eye, axis=0, keepdims=True)
 
     def weight_copy(k):
         return remote(
@@ -367,7 +378,8 @@
     inner = 2 if n_dp % 2 == 0 else 1
     line = n_dp // inner
     rows, emb = proj_query.shape
-    depth = query_feats.shape[2]
+    depth = n_dp * block
+    inside = query_feats.ndim == 2
     chunks = max(1, emb // 256)
     wide = emb // chunks
     bf16 = lambda *shape: pltpu.VMEM(shape, jnp.bfloat16)
@@ -378,7 +390,7 @@
         functools.partial(step_kernel, n_dp, n_group, inner, chunks),
         out_shape=(
             jax.ShapeDtypeStruct((block, emb), jnp.float32),
-            jax.ShapeDtypeStruct((rows, 1), jnp.float32),
+            jax.ShapeDtypeStruct((1, rows), jnp.float32),
         ),
         in_specs=[VMEM] * 6,
         out_specs=(VMEM, VMEM),
@@ -399,7 +411,8 @@
         + pairs(n_group) + pairs(n_dp) + pairs(2, n_group)
         + sems(2, 2, line) + sems(2, inner, line) + sems(2, n_dp) + pairs(2, n_group)
         + pairs(n_group) + pairs(n_dp)
-        + pairs(2, chunks, n_group) + pairs(chunks, inner) + pairs(chunks, line),
+        + pairs(2, chunks, n_group) + pairs(chunks, inner) + pairs(chunks, line)
+        + ([bf16(2, n_group, rows, depth)] if inside else []),
         compiler_params=pltpu.CompilerParams(has_side_effects=True, vmem_limit_bytes=67043328),
         name="step",
     )(proj_query, proj_pass, stats, query_feats, pass_feats, named)
@@ -413,6 +426,8 @@
     block = width // (n_dp * n_group)
 
     def cut(feats):
+        if block % 128 == 0:
+            return feats
         feats = feats.reshape(rows, n_dp, n_group, block)
         return feats.transpose(2, 0, 1, 3).reshape(n_group, rows, n_dp * block)
 

time: 131 us -> 128 us (0.977)
  local copies, waits for them, and re-layouts: 6.93 us -> 3.95 us
  other arithmetic: 2.75 us -> 1.29 us
    reshape x6 -> x0, local copies, waits for them, and re-layouts: 4.36 us -> none  [the longest x2 2.58 us: cut(): return feats.transpose(2, 0, 1, 3).reshape(n_group, rows, n_dp * block)]
    dot_general x1, matrix products: 2.06 us -> 6.01 us  [body(): jnp.dot(query_feats, head, preferred_element_type=jnp.float32)]
    dot_general x1, matrix products: 5.82 us -> 2.04 us  [body(): jnp.dot(passage_feats, head, preferred_element_type=jnp.float32)]
    pallas_call x1 -> x0, other arithmetic: 1.47 us -> none  [whole_step(): pl.pallas_call(functools.partial(step_kernel, n_dp, n_group, inner, chunk...]
    unnamed x10 -> x9, local copies, waits for them, and re-layouts: 2.58 us -> 3.95 us
where the time goes in v4:
time: 128 us; the launch traced here: 127 us
  Pallas kernels  113 us (88%)
  matrix products  8.05 us (6%)
  local copies, waits for them, and re-layouts  3.95 us (3%)
  other arithmetic  1.29 us (1%)
    pallas_call x1, Pallas kernels, whole_step(): pl.pallas_call(functools.partial(step_kernel, n_dp, n_group, inner, chunk...  113 us
    dot_general x1, matrix products, body(): jnp.dot(query_feats, head, preferred_element_type=jnp.float32)  6.01 us
    unnamed x9, local copies, waits for them, and re-layouts  3.95 us

profile of v4, /device:TPU:0, one launch (start us, length us, event | category | flops | bytes accessed | tf_op | source)
XLA Modules:
  0.0 126.7 jit_solution(12116769315665102307)
XLA Ops:
  0.6 0.0 copy-start
  0.6 0.9 copy.6
  1.5 0.0 slice-start
  1.5 0.7 fusion.2.named
  2.2 0.0 slice-start.1
  2.2 6.0 %fusion.6 = (bf16[1024]{0:T(1024)(128)(2,1)S(1)}, bf16[1024]{0:T(1024)(128)(2,1)S(1)}, bf16[128,1024]{1,0:T(8,128)(2,1)}) fusion(bf16[128,4096]{1,0:T(8,128)(2,1)} %query_feats.1, bf16[4096,1024]{1,0:T(8,128)(2,1)} %param.6), kind=kOutput, calls=%fused_computation.18 | convolution fusion | flops 1074132992 | bytes 9703424 | tf_op jit(solution)/shard_map/dot_general | solution.py:434
  8.2 0.0 copy-done
  8.2 0.0 slice-done
  8.2 0.0 slice-done.1
  8.2 2.0 %fusion.5 = (bf16[1024]{0:T(1024)(128)(2,1)S(1)}, bf16[1024]{0:T(1024)(128)(2,1)S(1)}, bf16[128,1024]{1,0:T(8,128)(2,1)}) fusion(bf16[128,4096]{1,0:T(8,128)(2,1)S(1)} %copy-done, bf16[4096,1024]{1,0:T(8,128)(2,1)S(1)} %bitcast.8), kind=kOutput, calls=%fused_computation.17 | convolution fusion | flops 1074132992 | bytes 9703424 | tf_op jit(solution)/shard_map/dot_general | solution.py:435
  10.3 0.6 pad_maximum_fusion.stats
  10.9 112.7 %step.1 = (f32[128,1024]{1,0:T(8,128)}, f32[1,128]{1,0:T(1,128)}) custom-call(bf16[128,1024]{1,0:T(8,128)(2,1)} %get-tuple-element.10.proj_query, bf16[128,1024]{1,0:T(8,128)(2,1)} %get-tuple-element.11.proj_pass, f32[2,1024]{1,0:T(2,128)} %pad_maximum_fusion.stats, bf16[128,4096]{1,0:T(8,128)(2,1)} %query_feats.1, bf16[128,4096]{1,0:T(8,128)(2,1)} %pass_feats.1, ...), custom_call_target="tpu_custom_call" | custom-call | tf_op jit(solution)/shard_map/step/pallas_call | solution.py:389
  123.6 1.9 %copy.12 = f32[128,1024]{1,0:T(8,128)} copy(f32[128,1024]{1,0:T(8,128)} %get-tuple-element.14) | data formatting | bytes 1048576
  125.5 1.2 copy.13
  (3 shorter events, 0.0 us)
Async XLA Ops:
  0.6 7.6 %copy-start = (bf16[128,4096]{1,0:T(8,128)(2,1)S(1)}, bf16[128,4096]{1,0:T(8,128)(2,1)}, u32[]{:S(2)}) copy-start(bf16[128,4096]{1,0:T(8,128)(2,1)} %pass_feats.1) | copy-start | bytes 3145732
  1.5 6.7 %slice-start = ((s8[8388608]{0:T(1024)(128)(4,1)}), s8[4194304]{0:T(1024)(128)(4,1)S(1)}, s32[]{:S(2)}) async-start(s8[8388608]{0:T(1024)(128)(4,1)} %bitcast.7), calls=%async_computation | async-start | bytes 8388608
  2.2 6.0 %slice-start.1 = ((s8[8388608]{0:T(1024)(128)(4,1)}), s8[4194304]{0:T(1024)(128)(4,1)S(1)}, s32[]{:S(2)}) async-start(s8[8388608]{0:T(1024)(128)(4,1)} %bitcast.7), calls=%async_computation.1 | async-start | bytes 8388608
